TPU v7x, 32 devices: a whole 2x2x4 slice. The times are simulated.
32 devices in a mesh: dp: 4 (over x, core), fsdp: 8 (over z, y).
Axes of the slice: x: 2, y: 2, z: 4, core: 2. Of those that a mesh axis runs over, the one named last changes fastest.
Arguments:
- tokens: bfloat16 [16384, 768], P(('dp', 'fsdp')), may hold values from -6 to 6
- seg_ids: int32 [16384], P(('dp', 'fsdp')), may hold values from 0 to 63, never falling along the last dimension, each value on 1 to 1024 neighbouring positions
- out_grad: bfloat16 [16384, 768], P(('dp', 'fsdp')), may hold values from -6 to 6
- first_gain: bfloat16 [768], P('fsdp'), may hold values from 0.5 to 1.5
- first_bias: bfloat16 [768], P('fsdp'), may hold values from -1.75 to 1.75
- second_gain: bfloat16 [768], P('fsdp'), may hold values from 0.5 to 1.5
- second_bias: bfloat16 [768], P('fsdp'), may hold values from -1.75 to 1.75
- qkv_weight: bfloat16 [768, 2304], P('fsdp'), may hold values from -0.21875 to 0.21875
- qkv_bias: bfloat16 [2304], P('fsdp'), may hold values from -1.75 to 1.75
- dense_weight: bfloat16 [768, 768], P('fsdp'), may hold values from -1.25 to 1.25
- up_weight: bfloat16 [768, 3072], P('fsdp'), may hold values from -0.21875 to 0.21875
- up_bias: bfloat16 [3072], P('fsdp'), may hold values from -1.75 to 1.75
- down_weight: bfloat16 [3072, 768], P('fsdp'), may hold values from -0.109375 to 0.109375
- out_bias: bfloat16 [768], P('fsdp'), may hold values from -1.75 to 1.75
Outputs:
- output: bfloat16 [16384, 768], P(('dp', 'fsdp'))
- input_grad: bfloat16 [16384, 768], P(('dp', 'fsdp'))
- first_gain_grad: float32 [768], P('fsdp')
- first_bias_grad: float32 [768], P('fsdp')
- second_gain_grad: float32 [768], P('fsdp')
- second_bias_grad: float32 [768], P('fsdp')
- qkv_weight_grad: float32 [768, 2304], P('fsdp')
- qkv_bias_grad: float32 [2304], P('fsdp')
- dense_weight_grad: float32 [768, 768], P('fsdp')
- up_weight_grad: float32 [768, 3072], P('fsdp')
- up_bias_grad: float32 [3072], P('fsdp')
- down_weight_grad: float32 [3072, 768], P('fsdp')
- out_bias_grad: float32 [768], P('fsdp')
- doc_norms: float32 [64], replicated
Inputs may be any that keep to these rules, and one draw needn't show every extreme that they name: seg_ids never falls along the stream; each document has 1 to 1024 tokens, one exactly 1024; every number below 64 occurs.
All inputs are finite; a program needn't handle non-finite values.
Results may differ from a plain program's by a relative error of at most 0.0093.
Values may be sent and summed in bfloat16 or wider, within the bound.
A program may use at most 128 MiB of HBM per device.

v0:
```python
import functools
import math

import jax
import jax.numpy as jnp
from jax import lax
from jax.experimental import pallas as pl
from jax.experimental.pallas import tpu as pltpu
from jax.sharding import PartitionSpec as P

D = 768
H = 12
HD = 64
FF = 3072
ROT = 16
ROW = 2048
DOC_DEV = 2
LANES = 128
PAIRS = D // LANES
MESH = pl.DeviceIdType.MESH
VMEM_LIMIT = 60 * 1024 * 1024


class Layout:
    def __init__(self, dp, fsdp):
        self.dp, self.fsdp = dp, fsdp
        self.nc = 2
        self.nx = dp // 2
        ny = 1
        while (2 * ny) * (2 * ny) <= fsdp:
            ny *= 2
        self.ny, self.nz = ny, fsdp // ny
        self.sub = max(1, self.nx // 2)
        self.unit = 4 // self.nx
        self.down_unit = 2 // self.sub

    def coords(self):
        d, f = lax.axis_index("dp"), lax.axis_index("fsdp")
        return d // 2, d % 2, f // self.ny, f % self.ny

    def device(self, x, c, z, y):
        return {"dp": x * 2 + c, "fsdp": z * self.ny + y}


def wrap(value, size):
    return lax.rem(value + size, size)


CHUNKS = tuple((g, i) for g in range(3) for i in range(3))
ALL = slice(None)


def grad_shape(lay, group, r):
    return (lay.nz, lay.ny, r, 4 * D) if group < 2 else (lay.nz, lay.ny, 4, r, D)


def span_of(lay, group, i, c, x):
    if group < 2:
        width = 512 // lay.nx
        if x is ALL:
            return pl.ds(pl.multiple_of(1024 * i + 512 * c, LANES), 512), None
        return pl.ds(pl.multiple_of(1024 * i + 512 * c + width * x, LANES), width), None
    width = 256 // lay.sub
    if x is ALL:
        return pl.ds(256 * i, 256), pl.ds(2 * c, 2)
    start = 256 * i + width * lax.rem(x, lay.sub)
    return pl.ds(pl.multiple_of(start, LANES), width), 2 * c + x // lay.sub


def view(lay, ref, group, i, c, x, z, y):
    cols, quarter = span_of(lay, group, i, c, x)
    if group < 2:
        return ref.at[z, y, :, cols]
    return ref.at[z, y, quarter, :, cols]


def shard_view(lay, ref, group, i, c, x):
    cols, quarter = span_of(lay, group, i, c, x)
    if group < 2:
        return ref.at[:, cols]
    return ref.at[quarter, :, cols]


def part_shape(lay, group, x_all, z_all, y_all, r):
    lead = ((lay.nz,) if z_all else ()) + ((lay.ny,) if y_all else ())
    if group < 2:
        return lead + (r, 512 if x_all else 512 // lay.nx)
    return lead + ((2, r, 256) if x_all else (r, 256 // lay.sub))


def barrier_with(peers):
    sem = pltpu.get_barrier_semaphore()
    for peer in peers:
        pl.semaphore_signal(sem, inc=1, device_id=peer, device_id_type=MESH)
    pl.semaphore_wait(sem, len(peers))


def line_peers(lay):
    x, c, z, y = lay.coords()
    xs = [lay.device(wrap(x + k, lay.nx), c, z, y) for k in range(1, lay.nx)]
    ys = [lay.device(x, c, z, wrap(y + k, lay.ny)) for k in range(1, lay.ny)]
    zs = [lay.device(x, c, wrap(z + k, lay.nz), y) for k in range(1, lay.nz)]
    cs = [lay.device(x, 1 - c, z, y)]
    return xs, cs, zs, ys


def remote(src, dst, ssem, rsem, device):
    return pltpu.make_async_remote_copy(
        src_ref=src, dst_ref=dst, send_sem=ssem, recv_sem=rsem, device_id=device, device_id_type=MESH
    )


def start(copies):
    for copy in copies:
        copy.start()


def arrive(copies):
    for copy in copies:
        copy.wait_recv()


def sent(copies):
    for copy in copies:
        copy.wait_send()


def hbm(count):
    return [pl.BlockSpec(memory_space=pltpu.HBM)] * count


def dma(*shape):
    return pltpu.SemaphoreType.DMA(shape)


NT = (((1,), (1,)), ((), ()))
NN = (((1,), (0,)), ((), ()))
F32 = jnp.float32
BF = jnp.bfloat16


def mm(a, b, dims=NN):
    return lax.dot_general(a, b, dims, preferred_element_type=F32)


def norm_parts(values):
    middle = jnp.mean(values, -1, keepdims=True)
    centred = values - middle
    factor = lax.rsqrt(jnp.mean(centred * centred, -1, keepdims=True) + 1e-05)
    return centred * factor, factor


class Gather:
    def __init__(self, lay, gs, sems):
        (z_s, z_r, y_s, y_r, x_s, x_r, c_s, c_r) = sems
        x, c, z, y = lay.coords()
        xs, cs, zs, ys = line_peers(lay)
        self.stages = []
        for t, (g, i) in enumerate(CHUNKS):
            by_y, by_x = (ys, y_s, y_r), (xs, x_s, x_r)
            first, second = (by_y, by_x) if i < 2 else (by_x, by_y)
            middle = (x, ALL, ALL) if i < 2 else (ALL, ALL, y)
            steps = [
                ((zs, z_s, z_r), (x, z, y)),
                (first, (x, ALL, y)),
                (second, middle),
            ]
            stages = []
            for (peers, ss, rs), (px, pz, py) in steps:
                piece = view(lay, gs[g], g, i, c, px, pz, py)
                stages.append(
                    [remote(piece, piece, ss.at[t, k], rs.at[t, k], p) for k, p in enumerate(peers)]
                )
            piece = view(lay, gs[g], g, i, c, ALL, ALL, ALL)
            stages.append([remote(piece, piece, c_s.at[t], c_r.at[t], cs[0])])
            self.stages.append(stages)

    def issue(self, t, stage):
        start(self.stages[t][stage])

    def pass_on(self, t, stage):
        arrive(self.stages[t][stage - 1])
        start(self.stages[t][stage])

    def done(self, t):
        arrive(self.stages[t][3])

    def drain(self):
        for stages in self.stages:
            for copies in stages:
                sent(copies)


def rope(u, cos, low, high):
    return u * cos + pltpu.roll(u, LANES - 8, 1) * low + pltpu.roll(u, 8, 1) * high


def front_kernel(
    lay, rows,
    u_att, u_up, u_down, small, tok, grad, seg,
    g_up, g_down, p_att, fg_prev, fg_own, attn_out, vectors, up_add, att_sums,
    g_att, g_small, tok_halo, seg_halo, first_all, first_t, q_s, k_s, v_s, do_s, ctx_s, ctx_t,
    dq_s, dk_s, dv_s, cos_s, low_s, high_s, bias, dk_acc, dv_acc, qkv_add,
    local_sem, z_s, z_r, y_s, y_r, x_s, x_r, c_s, c_r, sm_s, sm_r, h_s, h_r,
):
    span = 3 * rows
    r = u_att.shape[0]
    x, c, z, y = lay.coords()
    xs, cs, zs, ys = line_peers(lay)
    total = lay.dp * lay.fsdp
    b = lax.axis_index("dp") * lay.fsdp + lax.axis_index("fsdp")

    def stream(k):
        t = wrap(b + k, total)
        return {"dp": t // lay.fsdp, "fsdp": lax.rem(t, lay.fsdp)}

    around = [stream(2), stream(-2), stream(1), stream(-1)]
    barrier_with(xs + cs + zs + ys + around)
    gs = (g_att, g_up, g_down)
    us = (u_att, u_up, u_down)
    locals_ = [pltpu.make_async_copy(small, g_small.at[z, y], local_sem.at[9])]
    for t, (g, i) in enumerate(CHUNKS):
        locals_.append(
            pltpu.make_async_copy(
                shard_view(lay, us[g], g, i, c, x), view(lay, gs[g], g, i, c, x, z, y), local_sem.at[t]
            )
        )
    start(locals_)
    even = lax.rem(b, 2) == 0
    half = rows // 2
    halo, own, passed = [], [], []
    for k in range(2):
        part = pl.ds(k * half, half)
        halo.append(remote(tok.at[part], tok_halo.at[0, part], h_s.at[k], h_r.at[k], around[0]))
        own.append(remote(tok.at[part], tok_halo.at[1, part], h_s.at[2 + k], h_r.at[2 + k], around[2]))
        passed.append(
            remote(tok_halo.at[0, part], tok_halo.at[1, part], h_s.at[2 + k], h_r.at[2 + k], around[3])
        )
    segs = [
        remote(seg, seg_halo.at[0], h_s.at[4], h_r.at[4], around[0]),
        remote(seg, seg_halo.at[1], h_s.at[5], h_r.at[5], around[2]),
    ]
    small_z = [
        remote(g_small.at[z, y], g_small.at[z, y], sm_s.at[k], sm_r.at[k], p) for k, p in enumerate(zs)
    ]
    small_y = [
        remote(g_small.at[:, y], g_small.at[:, y], sm_s.at[lay.nz + k], sm_r.at[lay.nz + k], p)
        for k, p in enumerate(ys)
    ]
    net = Gather(lay, gs, (z_s, z_r, y_s, y_r, x_s, x_r, c_s, c_r))

    for copy in locals_:
        copy.wait()
    start(small_z)
    start(segs)
    for t in range(3):
        net.issue(t, 0)
    start(halo)

    @pl.when(even)
    def _():
        start(own)

    def norm_rows(values):
        return norm_parts(values.astype(F32))[0]

    normed = norm_rows(tok[...])
    net.pass_on(0, 1)
    arrive(small_z)
    start(small_y)

    def tables(k, carry):
        at = pl.ds(pl.multiple_of(k * 256, 256), 256)
        lane = lax.broadcasted_iota(jnp.int32, (256, LANES), 1) % HD
        row = lax.broadcasted_iota(jnp.int32, (256, LANES), 0) + k * 256
        place = lax.rem((b - 2) * rows + row + 4 * ROW, ROW).astype(F32)
        rate = jnp.exp((lane % 8).astype(F32) * (-math.log(10000.0) / 8.0))
        angle = place * rate
        sine = jnp.sin(angle)
        cos_s[at, :] = jnp.where(lane < ROT, jnp.cos(angle), 1.0)
        low_s[at, :] = jnp.where(lane < 8, -sine, 0.0)
        high_s[at, :] = jnp.where((lane >= 8) & (lane < ROT), sine, 0.0)
        return carry

    net.pass_on(1, 1)
    lax.fori_loop(0, span // 256, tables, 0)
    net.pass_on(2, 1)
    arrive(small_y)

    pieces = jnp.concatenate(
        [g_small[a, e] for a in range(lay.nz) for e in range(lay.ny)], 1
    )
    depth = lay.fsdp * LANES
    slot = lax.broadcasted_iota(jnp.int32, (depth, 256), 0)
    owner, lane_in = slot // LANES, slot % LANES
    inside = lane_in < r

    def place(row, count, per, offset, target, at):
        col = lax.broadcasted_iota(jnp.int32, (depth, 256), 1) + at
        hot = inside & (target(per * r * owner + offset * r + lane_in) == col)
        return mm(pieces[row : row + count], hot.astype(BF))

    def kinds(n):
        return ((n // HD) % 3) * D + (n // (3 * HD)) * HD + n % HD

    for j in range(3):
        vectors[:, 256 * j : 256 * (j + 1)] = place(0, 8, 1, 0, lambda n: n, 256 * j)
    net.pass_on(0, 2)

    def place_qkv(j, carry):
        at = pl.multiple_of(j * 256, 256)
        value = place(5, 1, 3, 0, kinds, at)
        for q in range(1, 3):
            value = value + place(5 + q, 1, 3, q, kinds, at)
        qkv_add[:, pl.ds(at, 256)] = value
        return carry

    lax.fori_loop(0, 9, place_qkv, 0)
    arrive([halo[0]])

    @pl.when(jnp.logical_not(even))
    def _():
        passed[0].start()

    net.pass_on(1, 2)
    net.pass_on(2, 2)

    def place_up(j, carry):
        at = pl.multiple_of(j * 256, 256)
        value = place(8, 1, 4, 0, lambda n: n, at)
        for q in range(1, 4):
            value = value + place(8 + q, 1, 4, q, lambda n: n, at)
        up_add[:, pl.ds(at, 256)] = value
        return carry

    lax.fori_loop(0, 12, place_up, 0)
    arrive([halo[1]])

    @pl.when(jnp.logical_not(even))
    def _():
        passed[1].start()

    net.issue(3, 0)
    net.issue(4, 0)
    gain, shift = vectors[0:1, :], vectors[1:2, :]
    own_rows = pl.ds(2 * rows, rows)
    first = (normed * gain + shift).astype(BF)
    first_all[own_rows, :] = first
    first_t[:, own_rows] = first.T

    arrive(segs)
    least = jnp.maximum(0, 2 * rows - b * rows)
    keys_doc = jnp.concatenate([seg_halo[0], seg_halo[1], seg[...]], 1).astype(F32)
    keys_doc = jnp.concatenate([keys_doc] * (LANES // 8), 0).T
    query_doc = seg[0:1, :].astype(F32)

    for k in range(6):
        at = slice(k * 256, (k + 1) * 256)
        key_at = lax.broadcasted_iota(jnp.int32, (256, rows), 0) + k * 256
        query_at = lax.broadcasted_iota(jnp.int32, (256, rows), 1) + 2 * rows
        allowed = (keys_doc[at, 0:1] == query_doc) & (key_at <= query_at) & (key_at >= least)
        bias[at, :] = jnp.where(allowed, 0.0, -1e30)
    net.pass_on(0, 3)
    net.pass_on(1, 3)
    net.pass_on(2, 3)
    net.issue(5, 0)
    for t in range(3):
        net.done(t)
    net.pass_on(3, 1)

    def weight(first_col, width):
        value = g_att[:, :, :, pl.ds(first_col, width)]
        return value.reshape(D, width)

    scale = 1.0 / math.sqrt(HD)
    do_s[...] = mm(grad[...], weight(3 * D, D), NT).astype(BF)

    def project(kind, j, at, out, factor):
        col = pl.multiple_of(kind * D + 256 * j, 256)
        value = mm(first_all[at, :], weight(col, 256)) + qkv_add[:, pl.ds(col, 256)]
        for k in range(2):
            u = value[:, k * LANES : (k + 1) * LANES]
            if kind < 2:
                u = rope(u, cos_s[at, :], low_s[at, :], high_s[at, :])
            if factor is not None:
                u = u * factor
            out[:, pl.ds(pl.multiple_of(256 * j + LANES * k, LANES), LANES)] = u.astype(BF)

    def own_projections(j, carry):
        project(0, j, own_rows, q_s, scale)
        project(1, j, own_rows, k_s.at[own_rows], None)
        project(2, j, own_rows, v_s.at[own_rows], None)
        return carry

    lax.fori_loop(0, 3, own_projections, 0)
    net.pass_on(4, 1)
    own[0].wait_recv()
    own[1].wait_recv()
    net.pass_on(5, 1)
    for k in range(2):
        at = slice(k * rows, (k + 1) * rows)
        before = (norm_rows(tok_halo[k]) * gain + shift).astype(BF)
        first_all[at, :] = before
        first_t[:, at] = before.T
    net.pass_on(3, 2)

    def earlier_projections(j, carry):
        for k in range(2):
            at = pl.ds(k * rows, rows)
            project(1, j, at, k_s.at[at], None)
            project(2, j, at, v_s.at[at], None)
        return carry

    lax.fori_loop(0, 3, earlier_projections, 0)
    net.issue(6, 0)
    net.pass_on(4, 2)

    later = [
        [lambda: net.pass_on(5, 2), lambda: net.issue(7, 0), lambda: net.pass_on(6, 1)],
        [lambda: net.pass_on(3, 3), lambda: net.issue(8, 0)],
        [lambda: net.pass_on(4, 3), lambda: net.pass_on(7, 1), lambda: net.pass_on(6, 2)],
        [lambda: net.pass_on(5, 3), lambda: net.pass_on(8, 1), lambda: net.pass_on(7, 2)],
        [lambda: net.pass_on(6, 3), lambda: net.pass_on(8, 2)],
        [lambda: net.pass_on(7, 3)],
    ]
    tile = 256

    def pair(p, carry):
        lanes = pl.ds(pl.multiple_of(p * LANES, LANES), LANES)
        v_pair, k_pair = v_s[:, lanes], k_s[:, lanes]
        v_t, k_t = v_pair.T, k_pair.T
        do_t = do_s[:, lanes].astype(F32).T
        lane = lax.broadcasted_iota(jnp.int32, (tile, LANES), 1)
        zero = jnp.zeros((), BF)
        for t in range(rows // tile):
            cols = slice(t * tile, (t + 1) * tile)
            kl = 2 * rows + (t + 1) * tile
            outs, dqs = [], []
            for hh in range(2):
                mine = (lane // HD) == hh
                qm = jnp.where(mine, q_s[cols, lanes], zero)
                dom = jnp.where(mine, do_s[cols, lanes], zero)
                st = mm(k_pair[:kl], qm, NT) + bias[:kl, cols]
                top = jnp.max(st, 0, keepdims=True)
                e = jnp.exp(st - top)
                w = e * (1.0 / jnp.sum(e, 0, keepdims=True))
                wb = w.astype(BF)
                part = slice(hh * HD, (hh + 1) * HD)
                o_t = mm(v_t[part, :kl], wb)
                delta = jnp.sum(o_t * do_t[part, cols], 0, keepdims=True)
                ds = (w * (mm(v_pair[:kl], dom, NT) - delta)).astype(BF)
                outs.append(o_t)
                dqs.append(mm(k_t[part, :kl], ds))
                dk_part, dv_part = mm(ds, qm), mm(wb, dom)
                if hh == 0 and t == 0:
                    dk_acc[:kl, :] = dk_part
                    dv_acc[:kl, :] = dv_part
                    dk_acc[kl:, :] = jnp.zeros((span - kl, LANES), F32)
                    dv_acc[kl:, :] = jnp.zeros((span - kl, LANES), F32)
                else:
                    dk_acc[:kl, :] += dk_part
                    dv_acc[:kl, :] += dv_part
            o_pair = jnp.concatenate(outs, 0)
            ctx_t[lanes, cols] = o_pair.astype(BF)
            ctx_s[cols, lanes] = o_pair.T.astype(BF)
            dq = jnp.concatenate(dqs, 0).T * scale
            at = slice(2 * rows + t * tile, 2 * rows + (t + 1) * tile)
            dq_s[cols, lanes] = rope(dq, cos_s[at, :], -low_s[at, :], -high_s[at, :]).astype(BF)
        dk_s[:, lanes] = rope(dk_acc[...], cos_s[...], -low_s[...], -high_s[...]).astype(BF)
        dv_s[:, lanes] = dv_acc[...].astype(BF)
        for k, events in enumerate(later):

            @pl.when(p == k)
            def _(events=events):
                for event in events:
                    event()

        return carry

    lax.fori_loop(0, PAIRS, pair, 0)
    net.pass_on(8, 3)

    def earlier_grad(k, carry):
        at = pl.ds(pl.multiple_of(k * 256, 256), 256)
        value = mm(dk_s[at, :], weight(D, D), NT) + mm(dv_s[at, :], weight(2 * D, D), NT)
        fg_prev[at, :] = value.astype(BF)
        return carry

    lax.fori_loop(0, 2 * rows // 256, earlier_grad, 0)
    for k in range(rows // 256):
        at = slice(2 * rows + 256 * k, 2 * rows + 256 * (k + 1))
        near = slice(256 * k, 256 * (k + 1))
        fg_own[near, :] = (
            mm(dk_s[at, :], weight(D, D), NT)
            + mm(dv_s[at, :], weight(2 * D, D), NT)
            + mm(dq_s[near, :], weight(0, D), NT)
        )

    def weight_grads(j, carry):
        col = pl.multiple_of(256 * j, 256)
        cols = pl.ds(col, 256)

        def put(kind, value):
            p_att[:, :, :, pl.ds(pl.multiple_of(kind * D + col, 256), 256)] = value.astype(BF).reshape(
                lay.nz, lay.ny, r, 256
            )

        put(0, mm(first_t[:, own_rows], dq_s[:, cols]))
        put(1, mm(first_t[...], dk_s[:, cols]))
        put(2, mm(first_t[...], dv_s[:, cols]))
        put(3, mm(ctx_t[...], grad[:, cols]))
        attn_out[:, cols] = mm(ctx_s[...], weight(pl.multiple_of(3 * D + col, 256), 256))
        return carry

    lax.fori_loop(0, 3, weight_grads, 0)
    for k, ref in enumerate((dq_s, dk_s, dv_s)):
        att_sums[k : k + 1, :] = jnp.sum(ref[...].astype(F32), 0, keepdims=True)
    att_sums[3:8, :] = jnp.zeros((5, D), F32)
    for t in range(3, 9):
        net.done(t)
    net.drain()
    sent(small_z + small_y + segs + halo + own)


def front(lay, u_att, u_up, u_down, small, tok, grad, seg):
    rows = tok.shape[0]
    span = 3 * rows
    r = u_att.shape[0]
    n = len(CHUNKS)
    outs = (
        jax.ShapeDtypeStruct(grad_shape(lay, 1, r), BF),
        jax.ShapeDtypeStruct(grad_shape(lay, 2, r), BF),
        jax.ShapeDtypeStruct(grad_shape(lay, 0, r), BF),
        jax.ShapeDtypeStruct((2 * rows, D), BF),
        jax.ShapeDtypeStruct((rows, D), F32),
        jax.ShapeDtypeStruct((rows, D), F32),
        jax.ShapeDtypeStruct((8, D), F32),
        jax.ShapeDtypeStruct((1, FF), F32),
        jax.ShapeDtypeStruct((8, D), F32),
    )
    vmem = pl.BlockSpec(memory_space=pltpu.VMEM)
    lx, ly, lz = max(1, lay.nx - 1), max(1, lay.ny - 1), max(1, lay.nz - 1)

    def v(shape, dtype=BF):
        return pltpu.VMEM(shape, dtype)

    return pl.pallas_call(
        functools.partial(front_kernel, lay, rows),
        name="front",
        out_shape=outs,
        in_specs=hbm(3) + [vmem] * 4,
        out_specs=tuple(hbm(2)) + (vmem,) * 7,
        scratch_shapes=[
            v(grad_shape(lay, 0, r)), v((lay.nz, lay.ny, 16, LANES)), v((2, rows, D)),
            v((2, 8, rows), jnp.int32), v((span, D)), v((D, span)), v((rows, D)), v((span, D)),
            v((span, D)), v((rows, D)), v((rows, D)), v((D, rows)), v((rows, D)), v((span, D)),
            v((span, D)), v((span, LANES), F32), v((span, LANES), F32), v((span, LANES), F32),
            v((span, rows), F32), v((span, LANES), F32), v((span, LANES), F32), v((1, 3 * D), F32),
            dma(n + 1), dma(n, lz), dma(n, lz), dma(n, ly), dma(n, ly), dma(n, lx), dma(n, lx),
            dma(n), dma(n), dma(lay.nz + ly), dma(lay.nz + ly), dma(6), dma(6),
        ],
        compiler_params=pltpu.CompilerParams(
            collective_id=0, has_side_effects=True, vmem_limit_bytes=VMEM_LIMIT
        ),
    )(u_att, u_up, u_down, small, tok, grad, seg)


class Reduce:
    def __init__(self, lay, ps, fs, bufs, sems):
        (ca, ra1, rb1, ra2, rb2, ra3) = bufs
        (c_s, c_r, x_s, x_r, y_s, y_r, z_s, z_r, fx_s, fx_r, fc_s, fc_r) = sems
        x, c, z, y = lay.coords()
        xs, cs, zs, ys = line_peers(lay)
        self.steps = []
        for t, (g, i) in enumerate(CHUNKS):
            p, f = ps[g], fs[g]
            other_x = [wrap(x + 1 + k, lay.nx) for k in range(lay.nx - 1)]
            other_y = [wrap(y + 1 + k, lay.ny) for k in range(lay.ny - 1)]
            other_z = [wrap(z + 1 + k, lay.nz) for k in range(lay.nz - 1)]

            def over_x(pieces, slot):
                return [
                    remote(piece, slot.at[k], x_s.at[t, k], x_r.at[t, k], xs[k])
                    for k, piece in enumerate(pieces)
                ]

            def over_y(pieces, slot):
                return [
                    remote(piece, slot.at[k], y_s.at[t, k], y_r.at[t, k], ys[k])
                    for k, piece in enumerate(pieces)
                ]

            def into(dst, slot, count):
                return functools.partial(add_into, dst, [slot.at[k] for k in range(count)])

            core_slot = ca[g].at[i]
            core = [
                remote(view(lay, p, g, i, 1 - c, ALL, ALL, ALL), core_slot, c_s.at[t], c_r.at[t], cs[0])
            ]
            add_core = functools.partial(add_into, view(lay, p, g, i, c, ALL, ALL, ALL), [core_slot])
            if i < 2:
                slot1, slot2 = ra1[g].at[i], ra2[g].at[i]
                first = over_x([view(lay, p, g, i, c, k, ALL, ALL) for k in other_x], slot1)
                add_1 = into(view(lay, p, g, i, c, x, ALL, ALL), slot1, lay.nx - 1)
                second = over_y([view(lay, p, g, i, c, x, ALL, k) for k in other_y], slot2)
                add_2 = into(view(lay, p, g, i, c, x, ALL, y), slot2, lay.ny - 1)
            else:
                slot1, slot2 = rb1[g].at[0], rb2[g].at[0]
                first = over_y([view(lay, p, g, i, c, ALL, ALL, k) for k in other_y], slot1)
                add_1 = into(view(lay, p, g, i, c, ALL, ALL, y), slot1, lay.ny - 1)
                second = over_x([view(lay, p, g, i, c, k, ALL, y) for k in other_x], slot2)
                add_2 = into(view(lay, p, g, i, c, x, ALL, y), slot2, lay.nx - 1)
            slot3 = ra3[g].at[i]
            third = [
                remote(view(lay, p, g, i, c, x, k, y), slot3.at[n], z_s.at[t, n], z_r.at[t, n], zs[n])
                for n, k in enumerate(other_z)
            ]
            out = shard_view(lay, f, g, i, c, x)
            own = view(lay, p, g, i, c, x, z, y)
            finish = functools.partial(
                set_sum, out, [own] + [slot3.at[k] for k in range(lay.nz - 1)]
            )
            share_x = [
                remote(out, out, fx_s.at[t, k], fx_r.at[t, k], peer) for k, peer in enumerate(xs)
            ]
            both = shard_view(lay, f, g, i, c, ALL)
            share_c = [remote(both, both, fc_s.at[t], fc_r.at[t], cs[0])]
            self.steps.append(
                (
                    (core, first, second, third, share_x, share_c),
                    (None, add_core, add_1, add_2, finish, None),
                )
            )

    def step(self, t, k):
        copies, adds = self.steps[t]
        if k > 0:
            arrive(copies[k - 1])
        if k < len(copies):
            if adds[k] is not None:
                adds[k]()
            start(copies[k])

    def drain(self):
        for copies, _ in self.steps:
            for group in copies:
                sent(group)


def set_sum(out, srcs):
    total = srcs[0][...].astype(F32)
    for src in srcs[1:]:
        total = total + src[...].astype(F32)
    out[...] = total.astype(BF)


def add_into(dst, srcs):
    lead = dst.shape[:-2]

    def body(j, carry):
        index = []
        rest = j
        for size in reversed(lead):
            index.append(lax.rem(rest, size))
            rest = rest // size
        index = tuple(reversed(index))
        total = dst[index].astype(F32)
        for src in srcs:
            total = total + src[index].astype(F32)
        dst[index] = total.astype(BF)
        return carry

    lax.fori_loop(0, math.prod(lead), body, 0)


def norm_back(grad, gain, normed, factor):
    inner = grad * gain
    return factor * (
        inner
        - jnp.mean(inner, -1, keepdims=True)
        - normed * jnp.mean(inner * normed, -1, keepdims=True)
    )


FF_CHUNKS = FF // D


def back_kernel(
    lay, rows, docs,
    g_up, g_down, p_att, fg_prev, fg_own, attn_out, vectors, up_add, att_sums, tok, grad, seg,
    output, input_grad, f_att, f_up, f_down, vec_out,
    p_up, p_down, w_up, w_down, second_in, second_t, act_s, pg_s, sg_acc, hop, home,
    ca, ra1, rb1, ra2, rb2, ra3, v_c, v_x, v_y, v_z, *sems,
):
    (c_s, c_r, x_s, x_r, y_s, y_r, z_s, z_r, fx_s, fx_r, fc_s, fc_r, v_s, v_r, w_sem, h_s, h_r) = sems
    r = p_att.shape[2]
    x, c, z, y = lay.coords()
    xs, cs, zs, ys = line_peers(lay)
    total = lay.dp * lay.fsdp
    b = lax.axis_index("dp") * lay.fsdp + lax.axis_index("fsdp")

    def stream(k):
        t = wrap(b + k, total)
        return {"dp": t // lay.fsdp, "fsdp": lax.rem(t, lay.fsdp)}

    around = [stream(2), stream(-2), stream(1), stream(-1)]
    near_z = lay.nz // FF_CHUNKS
    loads = []
    for k in range(FF_CHUNKS):
        slot = k % 2
        loads.append(
            (
                pltpu.make_async_copy(
                    g_up.at[:, :, :, pl.ds(D * k, D)], w_up.at[slot], w_sem.at[0, k]
                ),
                pltpu.make_async_copy(
                    g_down.at[pl.ds(near_z * k, near_z)], w_down.at[slot], w_sem.at[1, k]
                ),
            )
        )
    start(loads[0])
    start(loads[1])
    barrier_with(xs + cs + zs + ys + around)
    net = Reduce(
        lay, (p_att, p_up, p_down), (f_att, f_up, f_down), (ca, ra1, rb1, ra2, rb2, ra3), sems[:12]
    )
    for t in range(3):
        net.step(t, 0)
    even = lax.rem(b, 2) == 0
    one, two = fg_prev.at[pl.ds(rows, rows)], fg_prev.at[pl.ds(0, rows)]
    to_next = remote(one, hop, h_s.at[0], h_r.at[0], around[2])
    to_last = remote(one, hop, h_s.at[0], h_r.at[0], around[3])
    to_owner = remote(two, home, h_s.at[1], h_r.at[1], around[1])

    @pl.when(even)
    def _():
        to_next.start()
        to_owner.start()

    @pl.when(jnp.logical_not(even))
    def _():
        to_last.start()

    gain_first, gain_second = vectors[0:1, :], vectors[2:3, :]
    normed, factor = norm_parts(tok[...].astype(F32))
    value = (normed * gain_second + vectors[3:4, :]).astype(BF)
    second_in[...] = value
    second_t[...] = value.T
    cot = grad[...].astype(F32)
    output_base = attn_out
    output_base[...] = attn_out[...] + tok[...].astype(F32) + vectors[4:5, :]
    sg_acc[...] = jnp.zeros_like(sg_acc)
    mine = v_c.at[c]
    mine[...] = jnp.zeros((16, D), F32)
    for t in range(3):
        net.step(t, 1)

    events = [
        [(0, 2)],
        [(3, 0), (2, 2), (1, 2), (0, 3)],
        [(4, 0), (3, 1), (2, 3), (1, 3), (0, 4)],
        [(1, 4), (2, 4), (0, 5)],
    ]
    root = math.sqrt(0.5)
    level = 1.0 / math.sqrt(2.0 * math.pi)

    def forward_halo():
        to_last.wait_recv()

        @pl.when(jnp.logical_not(even))
        def _():
            add_into(two.reshape((2, rows // 2, D)), [hop.reshape((2, rows // 2, D))])
            to_owner.start()

    def chunk(k, squares):
        slot = lax.rem(k, 2)
        for n in range(FF_CHUNKS):

            @pl.when(k == n)
            def _(n=n):
                loads[n][0].wait()
                loads[n][1].wait()

        down = w_down[slot].reshape(D, D)
        for j in range(3):
            tile = slice(256 * j, 256 * (j + 1))
            col = pl.ds(pl.multiple_of(D * k + 256 * j, 256), 256)
            pre = mm(second_in[...], w_up[slot, :, :, :, tile].reshape(D, 256)) + up_add[:, col]
            hidden = mm(grad[...], down[tile, :], NT)
            half = 0.5 + 0.5 * lax.erf(pre * root)
            act = (pre * half).astype(BF)
            slope = half + pre * jnp.exp(-0.5 * pre * pre) * level
            pg = (hidden * slope).astype(BF)
            act_s[:, tile] = act
            pg_s[:, tile] = pg
            wide = act.astype(F32)
            squares = squares + jnp.sum(wide * wide, -1, keepdims=True)
            v_c[c, pl.ds(8 + k, 1), tile] = jnp.sum(pg.astype(F32), 0, keepdims=True)
        p_up[:, :, :, pl.ds(pl.multiple_of(D * k, 256), D)] = (
            mm(second_t[...], pg_s[...]).astype(BF).reshape(lay.nz, lay.ny, r, D)
        )
        p_down[pl.ds(near_z * k, near_z)] = (
            mm(act_s[...].T, grad[...]).astype(BF).reshape(near_z, lay.ny, 4, r, D)
        )
        output_base[...] += mm(act_s[...], down)
        sg_acc[...] += mm(pg_s[...], w_up[slot].reshape(D, D), NT)
        for n in range(FF_CHUNKS):

            @pl.when(k == n)
            def _(n=n):
                if n + 2 < FF_CHUNKS:
                    start(loads[n + 2])
                for event in events[n]:
                    net.step(*event)
                if n == 2:
                    forward_halo()

        return squares

    squares = lax.fori_loop(0, FF_CHUNKS, chunk, jnp.zeros((rows, 1), F32))
    net.step(5, 0)
    net.step(4, 1)
    net.step(3, 2)
    output[...] = output_base[...].astype(BF)
    net.step(6, 0)
    net.step(5, 1)
    net.step(7, 0)
    net.step(8, 0)

    to_owner.wait_recv()
    total_first = fg_own[...] + home[...].astype(F32)
    keep = jnp.where(even, 1.0, 0.0).astype(F32)
    fg_own[...] = total_first + hop[...].astype(F32) * keep
    first_grad = fg_own[...]
    second_grad = sg_acc[...]
    normed, factor = norm_parts(tok[...].astype(F32))
    input_grad[...] = (
        grad[...].astype(F32)
        + norm_back(first_grad, gain_first, normed, factor)
        + norm_back(second_grad, gain_second, normed, factor)
    ).astype(BF)
    net.step(4, 2)
    net.step(6, 1)

    def put(k, value):
        v_c[c, k : k + 1, :] = value

    put(0, jnp.sum(first_grad * normed, 0, keepdims=True))
    put(1, jnp.sum(first_grad, 0, keepdims=True))
    put(2, jnp.sum(second_grad * normed, 0, keepdims=True))
    put(3, jnp.sum(second_grad, 0, keepdims=True))
    cot = grad[...].astype(F32)
    put(4, jnp.sum(cot, 0, keepdims=True))
    for k in range(3):
        put(5 + k, att_sums[k : k + 1, :])
    token_norm = squares * jnp.sum(cot * cot, -1, keepdims=True) * (1.0 / (FF * D))
    docs_of = jnp.concatenate([seg[...].astype(F32)] * (LANES // 8), 0).T[:, 0:1]
    doc = lax.broadcasted_iota(jnp.int32, (rows, D), 1).astype(F32)
    member = jnp.where((docs_of == doc) & (doc < docs), 1.0, 0.0)
    put(12, jnp.sum(token_norm * member, 0, keepdims=True))
    put(13, jnp.sum(member, 0, keepdims=True))

    at = [0, 1, lay.nx, lay.nx + lay.ny - 1]

    def spread(ref, own, peers, base):
        return [
            remote(ref.at[own], ref.at[own], v_s.at[base + k], v_r.at[base + k], p)
            for k, p in enumerate(peers)
        ]

    vec_c = spread(v_c, c, cs, at[0])
    vec_x = spread(v_x, x, xs, at[1])
    vec_y = spread(v_y, y, ys, at[2])
    vec_z = spread(v_z, z, zs, at[3])

    def add_all(ref, size):
        value = ref[0]
        for k in range(1, size):
            value = value + ref[k]
        return value

    start(vec_c)
    net.step(3, 3)
    net.step(5, 2)
    arrive(vec_c)
    v_x[x] = add_all(v_c, 2)
    start(vec_x)
    net.step(7, 1)
    net.step(8, 1)
    net.step(4, 3)
    arrive(vec_x)
    v_y[y] = add_all(v_x, lay.nx)
    start(vec_y)
    net.step(5, 3)
    net.step(3, 4)
    net.step(6, 2)
    arrive(vec_y)
    v_z[z] = add_all(v_y, lay.ny)
    start(vec_z)
    net.step(4, 4)
    net.step(1, 5)
    net.step(2, 5)
    net.step(8, 2)
    net.step(6, 3)
    net.step(7, 2)
    arrive(vec_z)
    vec_out[...] = add_all(v_z, lay.nz)
    net.step(5, 4)
    net.step(3, 5)
    net.step(8, 3)
    net.step(7, 3)
    net.step(4, 5)
    net.step(5, 5)
    for t in (6, 8, 7):
        net.step(t, 4)
    for t in (6, 8, 7):
        net.step(t, 5)
    for t in range(9):
        net.step(t, 6)
    net.drain()
    sent(vec_c + vec_x + vec_y + vec_z)
    to_next.wait_send()
    to_owner.wait_send()


def back(lay, g_up, g_down, p_att, fg_prev, fg_own, attn_out, vectors, up_add, att_sums, tok, grad, seg):
    rows = tok.shape[0]
    r = p_att.shape[2]
    n = len(CHUNKS)
    docs = DOC_DEV * lay.dp * lay.fsdp
    outs = (
        jax.ShapeDtypeStruct((rows, D), BF),
        jax.ShapeDtypeStruct((rows, D), BF),
        jax.ShapeDtypeStruct((r, 4 * D), BF),
        jax.ShapeDtypeStruct((r, 4 * D), BF),
        jax.ShapeDtypeStruct((4, r, D), BF),
        jax.ShapeDtypeStruct((16, D), F32),
    )
    lx, ly, lz = max(1, lay.nx - 1), max(1, lay.ny - 1), max(1, lay.nz - 1)

    def v(shape, dtype=BF):
        return pltpu.VMEM(shape, dtype)

    def bufs(chunks, peers, x_all, z_all, y_all):
        return [v((chunks,) + peers + part_shape(lay, g, x_all, z_all, y_all, r)) for g in range(3)]

    scratch = [
        v(grad_shape(lay, 1, r)), v(grad_shape(lay, 2, r)),
        v((2, lay.nz, lay.ny, r, D)), v((2, lay.nz // FF_CHUNKS, lay.ny, 4, r, D)),
        v((rows, D)), v((D, rows)), v((rows, D)), v((rows, D)), v((rows, D), F32),
        v((rows, D)), v((rows, D)),
        bufs(3, (), True, True, True),
        bufs(2, (lx,), False, True, True),
        bufs(1, (ly,), True, True, False),
        bufs(2, (ly,), False, True, False),
        bufs(1, (lx,), False, True, False),
        bufs(3, (lz,), False, False, False),
    ]
    vecs = [v((k, 16, D), F32) for k in (2, lay.nx, lay.ny, lay.nz)]
    nv = 1 + lay.nx + lay.ny + lay.nz
    sems = [
        dma(n), dma(n), dma(n, lx), dma(n, lx), dma(n, ly), dma(n, ly), dma(n, lz), dma(n, lz),
        dma(n, lx), dma(n, lx), dma(n), dma(n), dma(nv), dma(nv), dma(2, FF_CHUNKS), dma(2), dma(2),
    ]
    vmem = pl.BlockSpec(memory_space=pltpu.VMEM)
    return pl.pallas_call(
        functools.partial(back_kernel, lay, rows, docs),
        name="back",
        out_shape=outs,
        in_specs=hbm(2) + [vmem] * 10,
        out_specs=(vmem,) * 6,
        scratch_shapes=scratch + vecs + sems,
        compiler_params=pltpu.CompilerParams(
            collective_id=1, has_side_effects=True, vmem_limit_bytes=VMEM_LIMIT
        ),
    )(g_up, g_down, p_att, fg_prev, fg_own, attn_out, vectors, up_add, att_sums, tok, grad, seg)


def per_device(
    lay, tokens, seg_ids, out_grad, first_gain, first_bias, second_gain, second_bias,
    qkv_weight, qkv_bias, dense_weight, up_weight, up_bias, down_weight, out_bias,
):
    rows = tokens.shape[0]
    r = qkv_weight.shape[0]
    fsdp = lay.fsdp
    qkv_kinds = qkv_weight.reshape(r, H, 3, HD).transpose(0, 2, 1, 3).reshape(r, 3 * D)
    u_att = jnp.concatenate([qkv_kinds, dense_weight], 1)
    u_down = down_weight.reshape(4, r, D)
    vectors = (first_gain, first_bias, second_gain, second_bias, out_bias, qkv_bias, up_bias)
    small = jnp.pad(jnp.concatenate(vectors).reshape(12, r), ((0, 4), (0, LANES - r)))
    seg_rows = jnp.broadcast_to(seg_ids[None, :], (8, rows))
    passed = front(lay, u_att, up_weight, u_down, small, tokens, out_grad, seg_rows)
    output, input_grad, f_att, f_up, f_down, vec = back(lay, *passed, tokens, out_grad, seg_rows)
    docs = DOC_DEV * lay.dp * fsdp
    shard = lax.axis_index("fsdp")
    plain = lax.dynamic_slice_in_dim(vec[:5], shard * r, r, 1)
    kinds = vec[5:8].reshape(3, H, HD).transpose(1, 0, 2).reshape(3 * D)
    qkv_add = lax.dynamic_slice_in_dim(kinds, shard * 3 * r, 3 * r)
    up_add = lax.dynamic_slice_in_dim(vec[8:12].reshape(FF), shard * 4 * r, 4 * r)
    qkv_out = (
        f_att[:, : 3 * D].astype(F32).reshape(r, 3, H, HD).transpose(0, 2, 1, 3).reshape(r, 3 * D)
    )
    return (
        output,
        input_grad,
        plain[0],
        plain[1],
        plain[2],
        plain[3],
        qkv_out,
        qkv_add,
        f_att[:, 3 * D :].astype(F32),
        f_up.astype(F32),
        up_add,
        f_down.reshape(4 * r, D).astype(F32),
        plain[4],
        vec[12, :docs] / vec[13, :docs],
    )


def solution(mesh):
    lay = Layout(mesh.shape["dp"], mesh.shape["fsdp"])
    both = P(("dp", "fsdp"))
    split = P("fsdp")
    in_specs = (both, both, both) + (split,) * 11
    out_specs = (both, both) + (split,) * 11 + (P(),)
    return jax.shard_map(
        functools.partial(per_device, lay), mesh=mesh, in_specs=in_specs, out_specs=out_specs,
        check_vma=False,
    )
```

profile of v0, /device:TPU:1, one launch (start us, length us, event | category | flops | bytes accessed | tf_op | source)
XLA Modules:
  0.0 321.8 jit_solution(17952201971416272253)
XLA Ops:
  0.6 1.3 broadcast_in_dim.2.seg
  1.9 1.3 copy.30
  3.3 0.0 copy-start.4
  3.3 0.0 copy-start.5
  3.3 0.0 copy-start.6
  3.3 0.0 copy-start.7
  3.4 0.0 copy-start.8
  3.4 0.0 copy-start.9
  3.4 0.0 copy-start.10
  3.4 0.0 copy-start.11
  3.4 0.2 copy.32
  3.6 0.5 copy-done.4
  4.2 0.9 pad_maximum_fusion.u_att
  5.0 0.0 copy-done.5
  5.0 0.0 copy-done.6
  5.0 0.0 copy-done.7
  5.0 0.0 copy-done.8
  5.1 0.0 copy-done.9
  5.1 0.0 copy-done.10
  5.1 0.0 copy-done.11
  5.1 0.1 concatenate.7
  5.2 0.1 reshape.67
  5.3 0.6 pad.4.small
  5.9 170.6 %front.1 = (bf16[4,2,96,3072]{3,2,1,0:T(8,128)(2,1)}, bf16[4,2,4,96,768]{4,3,2,1,0:T(8,128)(2,1)}, bf16[4,2,96,3072]{3,2,1,0:T(8,128)(2,1)}, bf16[1024,768]{1,0:...) custom-call(bf16[96,3072]{1,0:T(8,128)(2,1)} %pad_maximum_fusion.u_a, ...), custom_call_target="tpu_custom_call" | custom-call | tf_op jit(solution)/shard_map/front/pallas_call | solution.py:547
  176.4 130.9 %back.1 = (bf16[512,768]{1,0:T(8,128)(2,1)}, bf16[512,768]{1,0:T(8,128)(2,1)}, bf16[96,3072]{1,0:T(8,128)(2,1)}, bf16[96,3072]{1,0:T(8,128)(2,1)}, bf16[4,96,768]{2,1,0:T(8,128)(2,1)}, /*index=5*/f32[16,768]{1,0:T(8,128)}) custom-call(bf16[4,2,96,3072]{3,2,1,0:T(8,128)(2,1)} %get-tuple-element.29.g_up, bf16[4,2,4,96,768]{4,3,2,1,0:T(8,128)(2,1)} %get-tuple-element.30.g_down, ...), custom_call_target="tpu_custom_call" | custom-call | tf_op jit(solution)/shard_map/back/pallas_call | solution.py:966
  307.4 0.7 slice.42
  308.1 0.1 reshape.71
  308.2 0.1 reshape.72
  308.3 0.7 dynamic_slice.10
  308.9 0.7 slice.36
  309.7 0.1 constant_dynamic-slice_fusion
  309.7 0.5 slice_bitcast_fusion
  310.3 0.7 slice.44
  311.0 0.7 dynamic_slice.11
  311.7 1.3 fusion
  313.0 1.1 slice_convert_fusion
  314.0 0.4 copy.33
  314.4 0.1 copy.34
  314.5 0.0 copy-start.3
  314.5 1.3 copy.36
  315.8 1.7 slice_convert_fusion.1
  317.5 0.0 copy-done.3
  317.5 1.1 bitcast_convert_fusion
  318.7 1.1 convert_element_type.16
  319.8 0.3 copy-done.1
  320.1 0.9 copy.41
  321.0 0.0 copy-done
  321.0 0.9 copy.42
  (7 shorter events, 0.1 us)
Async XLA Ops:
  3.3 0.9 copy-start.4
  3.3 1.7 copy-start.5
  3.3 1.7 copy-start.6
  3.3 1.7 copy-start.7
  3.4 1.7 copy-start.8
  3.4 1.7 copy-start.9
  3.4 1.7 copy-start.10
  3.4 1.7 copy-start.11
  314.5 3.0 copy-start.3
  315.8 2.8 copy-start.2
  318.7 1.4 copy-start.1
  319.8 1.2 copy-start
where the time goes:
time: 322 us
  Pallas kernels  301 us (93%)
  local copies, waits for them, and re-layouts  12.4 us (4%)
  other arithmetic  7.16 us (2%)
    pallas_call x1, Pallas kernels, front(): pl.pallas_call(functools.partial(front_kernel, lay, rows), name='front',...  171 us
    pallas_call x1, Pallas kernels, back(): pl.pallas_call(functools.partial(back_kernel, lay, rows, docs), name='bac...  131 us

commit v1 on v0

--- a/solution.py
+++ b/solution.py
@@ -148,6 +148,24 @@
     centred = values - middle
     factor = lax.rsqrt(jnp.mean(centred * centred, -1, keepdims=True) + 1e-05)
     return centred * factor, factor
+
+
+def small_plan(r):
+    plan, at = [], 0
+    for size, within in [(r, LANES)] * 5 + [(3 * r, HD), (4 * r, LANES)]:
+        unit = math.gcd(size, within)
+        plan.append((at, size // unit, unit))
+        at += size // unit
+    return plan
+
+
+def pack_small(vectors, r):
+    rows = [
+        jnp.tile(v.reshape(-1, unit), (1, LANES // unit))
+        for v, (_, _, unit) in zip(vectors, small_plan(r))
+    ]
+    packed = jnp.concatenate(rows, 0).astype(F32)
+    return jnp.pad(packed, ((0, -packed.shape[0] % 8), (0, 0)))
 
 
 class Gather:
@@ -200,7 +218,7 @@
     u_att, u_up, u_down, small, tok, grad, seg,
     g_up, g_down, p_att, fg_prev, fg_own, attn_out, vectors, up_add, att_sums,
     g_att, g_small, tok_halo, seg_halo, first_all, first_t, q_s, k_s, v_s, do_s, ctx_s, ctx_t,
-    dq_s, dk_s, dv_s, cos_s, low_s, high_s, bias, dk_acc, dv_acc, qkv_add,
+    dq_s, dk_s, dv_s, cos_s, low_s, high_s, bias, dk_acc, dv_acc, qkv_add, s_s, w_s, d_s,
     local_sem, z_s, z_r, y_s, y_r, x_s, x_r, c_s, c_r, sm_s, sm_r, h_s, h_r,
 ):
     span = 3 * rows
@@ -287,35 +305,37 @@
     net.pass_on(2, 1)
     arrive(small_y)
 
-    pieces = jnp.concatenate(
-        [g_small[a, e] for a in range(lay.nz) for e in range(lay.ny)], 1
-    )
-    depth = lay.fsdp * LANES
-    slot = lax.broadcasted_iota(jnp.int32, (depth, 256), 0)
-    owner, lane_in = slot // LANES, slot % LANES
-    inside = lane_in < r
-
-    def place(row, count, per, offset, target, at):
-        col = lax.broadcasted_iota(jnp.int32, (depth, 256), 1) + at
-        hot = inside & (target(per * r * owner + offset * r + lane_in) == col)
-        return mm(pieces[row : row + count], hot.astype(BF))
-
-    def kinds(n):
-        return ((n // HD) % 3) * D + (n // (3 * HD)) * HD + n % HD
-
-    for j in range(3):
-        vectors[:, 256 * j : 256 * (j + 1)] = place(0, 8, 1, 0, lambda n: n, 256 * j)
+    lane_row = lax.broadcasted_iota(jnp.int32, (1, LANES), 1)
+
+    def line(first_row, per, unit, length, source):
+        out = []
+        for block in range(length // LANES):
+            value = None
+            for k in range(LANES // unit):
+                at = source(block * (LANES // unit) + k)
+                owner = at // per
+                row = first_row + at % per
+                piece = g_small[owner // lay.ny, owner % lay.ny, row : row + 1, :]
+                value = piece if value is None else jnp.where(lane_row // unit == k, piece, value)
+            out.append(value)
+        return jnp.concatenate(out, 1)
+
+    plan = small_plan(r)
+    for j in range(5):
+        vectors[j : j + 1, :] = line(*plan[j], D, lambda n: n)
+    vectors[5:8, :] = jnp.zeros((3, D), F32)
+    unit = plan[5][2]
+    a_head = HD // unit
+
+    def natural(n):
+        kind, rest = divmod(n, D // unit)
+        head, part = divmod(rest, a_head)
+        return head * 3 * a_head + kind * a_head + part
+
+    qkv_add[...] = line(*plan[5], 3 * D, natural)
+    up_add[...] = line(*plan[6], FF, lambda n: n)
     net.pass_on(0, 2)
 
-    def place_qkv(j, carry):
-        at = pl.multiple_of(j * 256, 256)
-        value = place(5, 1, 3, 0, kinds, at)
-        for q in range(1, 3):
-            value = value + place(5 + q, 1, 3, q, kinds, at)
-        qkv_add[:, pl.ds(at, 256)] = value
-        return carry
-
-    lax.fori_loop(0, 9, place_qkv, 0)
     arrive([halo[0]])
 
     @pl.when(jnp.logical_not(even))
@@ -325,15 +345,6 @@
     net.pass_on(1, 2)
     net.pass_on(2, 2)
 
-    def place_up(j, carry):
-        at = pl.multiple_of(j * 256, 256)
-        value = place(8, 1, 4, 0, lambda n: n, at)
-        for q in range(1, 4):
-            value = value + place(8 + q, 1, 4, q, lambda n: n, at)
-        up_add[:, pl.ds(at, 256)] = value
-        return carry
-
-    lax.fori_loop(0, 12, place_up, 0)
     arrive([halo[1]])
 
     @pl.when(jnp.logical_not(even))
@@ -427,39 +438,55 @@
 
     def pair(p, carry):
         lanes = pl.ds(pl.multiple_of(p * LANES, LANES), LANES)
-        v_pair, k_pair = v_s[:, lanes], k_s[:, lanes]
-        v_t, k_t = v_pair.T, k_pair.T
+        v_t, k_t = v_s[:, lanes].T, k_s[:, lanes].T
         do_t = do_s[:, lanes].astype(F32).T
         lane = lax.broadcasted_iota(jnp.int32, (tile, LANES), 1)
         zero = jnp.zeros((), BF)
         for t in range(rows // tile):
             cols = slice(t * tile, (t + 1) * tile)
             kl = 2 * rows + (t + 1) * tile
+            pieces = [slice(k * tile, (k + 1) * tile) for k in range(kl // tile)]
+            qms = [jnp.where((lane // HD) == hh, q_s[cols, lanes], zero) for hh in range(2)]
+            doms = [jnp.where((lane // HD) == hh, do_s[cols, lanes], zero) for hh in range(2)]
+            tops, norms = [], []
+            for hh in range(2):
+                top = None
+                for at in pieces:
+                    st = mm(k_s[at, lanes], qms[hh], NT) + bias[at, cols]
+                    s_s[hh, at, :] = st
+                    most = jnp.max(st, 0, keepdims=True)
+                    top = most if top is None else jnp.maximum(top, most)
+                tops.append(top)
+            for hh in range(2):
+                total_e = None
+                for at in pieces:
+                    e = jnp.exp(s_s[hh, at, :] - tops[hh])
+                    s_s[hh, at, :] = e
+                    part = jnp.sum(e, 0, keepdims=True)
+                    total_e = part if total_e is None else total_e + part
+                norms.append(1.0 / total_e)
             outs, dqs = [], []
             for hh in range(2):
-                mine = (lane // HD) == hh
-                qm = jnp.where(mine, q_s[cols, lanes], zero)
-                dom = jnp.where(mine, do_s[cols, lanes], zero)
-                st = mm(k_pair[:kl], qm, NT) + bias[:kl, cols]
-                top = jnp.max(st, 0, keepdims=True)
-                e = jnp.exp(st - top)
-                w = e * (1.0 / jnp.sum(e, 0, keepdims=True))
-                wb = w.astype(BF)
+                for at in pieces:
+                    w_s[hh, at, :] = (s_s[hh, at, :] * norms[hh]).astype(BF)
+            for hh in range(2):
                 part = slice(hh * HD, (hh + 1) * HD)
-                o_t = mm(v_t[part, :kl], wb)
+                o_t = mm(v_t[part, :kl], w_s[hh, :kl, :])
                 delta = jnp.sum(o_t * do_t[part, cols], 0, keepdims=True)
-                ds = (w * (mm(v_pair[:kl], dom, NT) - delta)).astype(BF)
                 outs.append(o_t)
-                dqs.append(mm(k_t[part, :kl], ds))
-                dk_part, dv_part = mm(ds, qm), mm(wb, dom)
-                if hh == 0 and t == 0:
-                    dk_acc[:kl, :] = dk_part
-                    dv_acc[:kl, :] = dv_part
-                    dk_acc[kl:, :] = jnp.zeros((span - kl, LANES), F32)
-                    dv_acc[kl:, :] = jnp.zeros((span - kl, LANES), F32)
+                for at in pieces:
+                    dp = mm(v_s[at, lanes], doms[hh], NT)
+                    d_s[hh, at, :] = ((s_s[hh, at, :] * norms[hh]) * (dp - delta)).astype(BF)
+                dqs.append(mm(k_t[part, :kl], d_s[hh, :kl, :]))
+            for k, at in enumerate(pieces):
+                dk = mm(d_s[0, at, :], qms[0]) + mm(d_s[1, at, :], qms[1])
+                dv = mm(w_s[0, at, :], doms[0]) + mm(w_s[1, at, :], doms[1])
+                if t == 0 or k == len(pieces) - 1:
+                    dk_acc[at, :] = dk
+                    dv_acc[at, :] = dv
                 else:
-                    dk_acc[:kl, :] += dk_part
-                    dv_acc[:kl, :] += dv_part
+                    dk_acc[at, :] += dk
+                    dv_acc[at, :] += dv
             o_pair = jnp.concatenate(outs, 0)
             ctx_t[lanes, cols] = o_pair.astype(BF)
             ctx_s[cols, lanes] = o_pair.T.astype(BF)
@@ -551,11 +578,12 @@
         in_specs=hbm(3) + [vmem] * 4,
         out_specs=tuple(hbm(2)) + (vmem,) * 7,
         scratch_shapes=[
-            v(grad_shape(lay, 0, r)), v((lay.nz, lay.ny, 16, LANES)), v((2, rows, D)),
+            v(grad_shape(lay, 0, r)), v((lay.nz, lay.ny) + small.shape, F32), v((2, rows, D)),
             v((2, 8, rows), jnp.int32), v((span, D)), v((D, span)), v((rows, D)), v((span, D)),
             v((span, D)), v((rows, D)), v((rows, D)), v((D, rows)), v((rows, D)), v((span, D)),
             v((span, D)), v((span, LANES), F32), v((span, LANES), F32), v((span, LANES), F32),
             v((span, rows), F32), v((span, LANES), F32), v((span, LANES), F32), v((1, 3 * D), F32),
+            v((2, span, 256), F32), v((2, span, 256)), v((2, span, 256)),
             dma(n + 1), dma(n, lz), dma(n, lz), dma(n, ly), dma(n, ly), dma(n, lx), dma(n, lx),
             dma(n), dma(n), dma(lay.nz + ly), dma(lay.nz + ly), dma(6), dma(6),
         ],
@@ -752,14 +780,14 @@
     sg_acc[...] = jnp.zeros_like(sg_acc)
     mine = v_c.at[c]
     mine[...] = jnp.zeros((16, D), F32)
-    for t in range(3):
-        net.step(t, 1)
+    net.step(0, 1)
+    net.step(1, 1)
 
     events = [
-        [(0, 2)],
-        [(3, 0), (2, 2), (1, 2), (0, 3)],
-        [(4, 0), (3, 1), (2, 3), (1, 3), (0, 4)],
-        [(1, 4), (2, 4), (0, 5)],
+        [(2, 1)],
+        [(3, 0), (0, 2)],
+        [(4, 0), (3, 1), (2, 2), (0, 3)],
+        [(4, 1), (1, 2), (5, 0)],
     ]
     root = math.sqrt(0.5)
     level = 1.0 / math.sqrt(2.0 * math.pi)
@@ -818,14 +846,11 @@
         return squares
 
     squares = lax.fori_loop(0, FF_CHUNKS, chunk, jnp.zeros((rows, 1), F32))
-    net.step(5, 0)
-    net.step(4, 1)
-    net.step(3, 2)
+    for t in (7, 8, 6):
+        net.step(t, 0)
     output[...] = output_base[...].astype(BF)
-    net.step(6, 0)
-    net.step(5, 1)
-    net.step(7, 0)
-    net.step(8, 0)
+    for t, k in ((3, 2), (0, 4), (1, 3), (5, 1), (7, 1), (8, 1), (6, 1), (2, 3)):
+        net.step(t, k)
 
     to_owner.wait_recv()
     total_first = fg_own[...] + home[...].astype(F32)
@@ -839,8 +864,8 @@
         + norm_back(first_grad, gain_first, normed, factor)
         + norm_back(second_grad, gain_second, normed, factor)
     ).astype(BF)
-    net.step(4, 2)
-    net.step(6, 1)
+    for t, k in ((3, 3), (1, 4), (4, 2), (2, 4), (0, 5)):
+        net.step(t, k)
 
     def put(k, value):
         v_c[c, k : k + 1, :] = value
@@ -880,41 +905,27 @@
         return value
 
     start(vec_c)
-    net.step(3, 3)
     net.step(5, 2)
+    net.step(3, 4)
     arrive(vec_c)
     v_x[x] = add_all(v_c, 2)
     start(vec_x)
-    net.step(7, 1)
-    net.step(8, 1)
-    net.step(4, 3)
+    for t, k in ((7, 2), (8, 2), (4, 3), (6, 2), (1, 5), (2, 5)):
+        net.step(t, k)
     arrive(vec_x)
     v_y[y] = add_all(v_x, lay.nx)
     start(vec_y)
-    net.step(5, 3)
-    net.step(3, 4)
-    net.step(6, 2)
+    for t, k in ((7, 3), (4, 4), (5, 3)):
+        net.step(t, k)
     arrive(vec_y)
     v_z[z] = add_all(v_y, lay.ny)
     start(vec_z)
-    net.step(4, 4)
-    net.step(1, 5)
-    net.step(2, 5)
-    net.step(8, 2)
-    net.step(6, 3)
-    net.step(7, 2)
+    for t, k in ((6, 3), (3, 5), (7, 4), (8, 3), (4, 5), (5, 4)):
+        net.step(t, k)
     arrive(vec_z)
     vec_out[...] = add_all(v_z, lay.nz)
-    net.step(5, 4)
-    net.step(3, 5)
-    net.step(8, 3)
-    net.step(7, 3)
-    net.step(4, 5)
-    net.step(5, 5)
-    for t in (6, 8, 7):
-        net.step(t, 4)
-    for t in (6, 8, 7):
-        net.step(t, 5)
+    for t, k in ((7, 5), (5, 5), (6, 4), (8, 4), (6, 5), (8, 5)):
+        net.step(t, k)
     for t in range(9):
         net.step(t, 6)
     net.drain()
@@ -987,7 +998,7 @@
     u_att = jnp.concatenate([qkv_kinds, dense_weight], 1)
     u_down = down_weight.reshape(4, r, D)
     vectors = (first_gain, first_bias, second_gain, second_bias, out_bias, qkv_bias, up_bias)
-    small = jnp.pad(jnp.concatenate(vectors).reshape(12, r), ((0, 4), (0, LANES - r)))
+    small = pack_small(vectors, r)
     seg_rows = jnp.broadcast_to(seg_ids[None, :], (8, rows))
     passed = front(lay, u_att, up_weight, u_down, small, tokens, out_grad, seg_rows)
     output, input_grad, f_att, f_up, f_down, vec = back(lay, *passed, tokens, out_grad, seg_rows)

time: 322 us -> 289 us (0.90)
  Pallas kernels: 301 us -> 265 us
    pallas_call x1, Pallas kernels: 171 us -> 143 us  [front(): pl.pallas_call(functools.partial(front_kernel, lay, rows), name='front',...]
    pallas_call x1, Pallas kernels: 131 us -> 122 us  [back(): pl.pallas_call(functools.partial(back_kernel, lay, rows, docs), name='bac...]
where the time goes in v1:
time: 289 us; the launch traced here: 286 us
  Pallas kernels  265 us (92%)
  local copies, waits for them, and re-layouts  13 us (4%)
  other arithmetic  7.77 us (3%)
    pallas_call x1, Pallas kernels, front(): pl.pallas_call(functools.partial(front_kernel, lay, rows), name='front',...  143 us
    pallas_call x1, Pallas kernels, back(): pl.pallas_call(functools.partial(back_kernel, lay, rows, docs), name='bac...  122 us

profile of v1, /device:TPU:1, one launch (start us, length us, event | category | flops | bytes accessed | tf_op | source)
XLA Modules:
  0.0 286.4 jit_solution(2915073729538940166)
XLA Ops:
  0.6 1.3 broadcast_in_dim.2.seg
  1.9 1.3 copy.30
  3.3 0.0 copy-start.4
  3.3 0.0 copy-start.5
  3.3 0.0 copy-start.7
  3.3 0.0 copy-start.8
  3.4 0.0 copy-start.10
  3.4 0.0 copy-start.11
  3.4 0.2 copy.32
  3.6 0.5 copy-done.4
  4.2 0.9 pad_maximum_fusion.u_att
  5.0 0.1 tile.75
  5.1 0.1 tile.77
  5.2 0.1 tile.60
  5.3 0.1 tile.62
  5.4 0.1 tile.63
  5.5 0.1 tile.65
  5.6 0.1 tile.66
  5.7 0.1 tile.68
  5.8 0.1 tile.69
  5.9 0.1 tile.71
  6.0 0.1 tile.72
  6.1 0.1 tile.74
  6.1 0.3 concatenate.7
  6.4 0.6 pad_convert_fusion.small
  7.1 143.2 %front.1 = (bf16[4,2,96,3072]{3,2,1,0:T(8,128)(2,1)}, bf16[4,2,4,96,768]{4,3,2,1,0:T(8,128)(2,1)}, bf16[4,2,96,3072]{3,2,1,0:T(8,128)(2,1)}, bf16[1024,768]{1,0:...) custom-call(bf16[96,3072]{1,0:T(8,128)(2,1)} %pad_maximum_fusion.u_a, ...), custom_call_target="tpu_custom_call" | custom-call | tf_op jit(solution)/shard_map/front/pallas_call | solution.py:574
  150.2 121.7 %back.1 = (bf16[512,768]{1,0:T(8,128)(2,1)}, bf16[512,768]{1,0:T(8,128)(2,1)}, bf16[96,3072]{1,0:T(8,128)(2,1)}, bf16[96,3072]{1,0:T(8,128)(2,1)}, bf16[4,96,768]{2,1,0:T(8,128)(2,1)}, /*index=5*/f32[16,768]{1,0:T(8,128)}) custom-call(bf16[4,2,96,3072]{3,2,1,0:T(8,128)(2,1)} %get-tuple-element.29.g_up, bf16[4,2,4,96,768]{4,3,2,1,0:T(8,128)(2,1)} %get-tuple-element.30.g_down, ...), custom_call_target="tpu_custom_call" | custom-call | tf_op jit(solution)/shard_map/back/pallas_call | solution.py:977
  271.9 0.7 slice.36
  272.7 0.1 constant_dynamic-slice_fusion
  272.8 0.5 slice_bitcast_fusion
  273.3 0.7 slice.42
  274.0 0.1 reshape.91
  274.1 0.1 reshape.92
  274.2 0.7 dynamic_slice.10
  274.9 0.7 slice.44
  275.6 0.7 dynamic_slice.11
  276.3 1.3 fusion
  277.5 1.1 slice_convert_fusion
  278.6 0.4 copy.33
  279.0 0.1 copy.34
  279.1 1.3 copy.36
  280.4 1.7 slice_convert_fusion.1
  282.1 1.1 bitcast_convert_fusion
  283.2 1.1 convert_element_type.17
  284.4 0.3 copy-done.1
  284.7 0.9 copy.41
  285.5 0.0 copy-done
  285.6 0.9 copy.42
  (24 shorter events, 0.1 us)
Async XLA Ops:
  3.3 0.9 copy-start.4
  3.3 1.7 copy-start.5
  3.3 1.9 copy-start.7
  3.3 2.1 copy-start.8
  3.4 2.2 copy-start.9
  3.4 2.4 copy-start.10
  3.4 2.6 copy-start.11
  3.4 2.8 copy-start.6
  279.1 3.0 %copy-start.3 = (bf16[4,96,768]{2,1,0:T(8,128)(2,1)S(1)}, bf16[4,96,768]{2,1,0:T(8,128)(2,1)}, u32[]{:S(2)}) copy-start(bf16[4,96,768]{2,1,0:T(8,128)(2,1)} %get-tuple-element.43) | copy-start | bytes 1769476
  280.4 2.8 copy-start.2
  283.2 1.4 copy-start.1
  284.4 1.2 copy-start

commit v2 on v1

--- a/solution.py
+++ b/solution.py
@@ -169,7 +169,7 @@
 
 
 class Gather:
-    def __init__(self, lay, gs, sems):
+    def __init__(self, lay, us, gs, sems):
         (z_s, z_r, y_s, y_r, x_s, x_r, c_s, c_r) = sems
         x, c, z, y = lay.coords()
         xs, cs, zs, ys = line_peers(lay)
@@ -186,8 +186,9 @@
             stages = []
             for (peers, ss, rs), (px, pz, py) in steps:
                 piece = view(lay, gs[g], g, i, c, px, pz, py)
+                source = shard_view(lay, us[g], g, i, c, x) if len(stages) == 0 else piece
                 stages.append(
-                    [remote(piece, piece, ss.at[t, k], rs.at[t, k], p) for k, p in enumerate(peers)]
+                    [remote(source, piece, ss.at[t, k], rs.at[t, k], p) for k, p in enumerate(peers)]
                 )
             piece = view(lay, gs[g], g, i, c, ALL, ALL, ALL)
             stages.append([remote(piece, piece, c_s.at[t], c_r.at[t], cs[0])])
@@ -223,6 +224,7 @@
 ):
     span = 3 * rows
     r = u_att.shape[0]
+    n_chunks = len(CHUNKS)
     x, c, z, y = lay.coords()
     xs, cs, zs, ys = line_peers(lay)
     total = lay.dp * lay.fsdp
@@ -233,17 +235,18 @@
         return {"dp": t // lay.fsdp, "fsdp": lax.rem(t, lay.fsdp)}
 
     around = [stream(2), stream(-2), stream(1), stream(-1)]
-    barrier_with(xs + cs + zs + ys + around)
     gs = (g_att, g_up, g_down)
     us = (u_att, u_up, u_down)
-    locals_ = [pltpu.make_async_copy(small, g_small.at[z, y], local_sem.at[9])]
+    locals_ = []
     for t, (g, i) in enumerate(CHUNKS):
         locals_.append(
             pltpu.make_async_copy(
                 shard_view(lay, us[g], g, i, c, x), view(lay, gs[g], g, i, c, x, z, y), local_sem.at[t]
             )
         )
+    locals_.append(pltpu.make_async_copy(small, g_small.at[z, y], local_sem.at[n_chunks]))
     start(locals_)
+    barrier_with(xs + cs + zs + ys + around)
     even = lax.rem(b, 2) == 0
     half = rows // 2
     halo, own, passed = [], [], []
@@ -259,33 +262,18 @@
         remote(seg, seg_halo.at[1], h_s.at[5], h_r.at[5], around[2]),
     ]
     small_z = [
-        remote(g_small.at[z, y], g_small.at[z, y], sm_s.at[k], sm_r.at[k], p) for k, p in enumerate(zs)
+        remote(small, g_small.at[z, y], sm_s.at[k], sm_r.at[k], p) for k, p in enumerate(zs)
     ]
     small_y = [
         remote(g_small.at[:, y], g_small.at[:, y], sm_s.at[lay.nz + k], sm_r.at[lay.nz + k], p)
         for k, p in enumerate(ys)
     ]
-    net = Gather(lay, gs, (z_s, z_r, y_s, y_r, x_s, x_r, c_s, c_r))
-
-    for copy in locals_:
-        copy.wait()
+    net = Gather(lay, us, gs, (z_s, z_r, y_s, y_r, x_s, x_r, c_s, c_r))
+    net.issue(0, 0)
+    net.issue(2, 0)
     start(small_z)
     start(segs)
-    for t in range(3):
-        net.issue(t, 0)
-    start(halo)
-
-    @pl.when(even)
-    def _():
-        start(own)
-
-    def norm_rows(values):
-        return norm_parts(values.astype(F32))[0]
-
-    normed = norm_rows(tok[...])
-    net.pass_on(0, 1)
-    arrive(small_z)
-    start(small_y)
+    net.issue(1, 0)
 
     def tables(k, carry):
         at = pl.ds(pl.multiple_of(k * 256, 256), 256)
@@ -300,10 +288,21 @@
         high_s[at, :] = jnp.where((lane >= 8) & (lane < ROT), sine, 0.0)
         return carry
 
+    lax.fori_loop(0, 2, tables, 0)
+    for t in (0, 2, 1, n_chunks):
+        locals_[t].wait()
+    net.pass_on(0, 1)
+    lax.fori_loop(2, 3, tables, 0)
+    net.pass_on(2, 1)
+    lax.fori_loop(3, 5, tables, 0)
+    arrive(small_z)
+    start(small_y)
+    net.pass_on(0, 2)
     net.pass_on(1, 1)
-    lax.fori_loop(0, span // 256, tables, 0)
-    net.pass_on(2, 1)
+    halo[0].start()
+    lax.fori_loop(5, span // 256, tables, 0)
     arrive(small_y)
+    net.pass_on(2, 2)
 
     lane_row = lax.broadcasted_iota(jnp.int32, (1, LANES), 1)
 
@@ -320,6 +319,9 @@
             out.append(value)
         return jnp.concatenate(out, 1)
 
+    def norm_rows(values):
+        return norm_parts(values.astype(F32))[0]
+
     plan = small_plan(r)
     for j in range(5):
         vectors[j : j + 1, :] = line(*plan[j], D, lambda n: n)
@@ -333,32 +335,27 @@
         return head * 3 * a_head + kind * a_head + part
 
     qkv_add[...] = line(*plan[5], 3 * D, natural)
+    net.pass_on(1, 2)
     up_add[...] = line(*plan[6], FF, lambda n: n)
-    net.pass_on(0, 2)
-
-    arrive([halo[0]])
-
-    @pl.when(jnp.logical_not(even))
-    def _():
-        passed[0].start()
-
-    net.pass_on(1, 2)
-    net.pass_on(2, 2)
-
-    arrive([halo[1]])
-
-    @pl.when(jnp.logical_not(even))
-    def _():
-        passed[1].start()
-
-    net.issue(3, 0)
-    net.issue(4, 0)
+
+    def pass_halo(k):
+        arrive([halo[k]])
+
+        @pl.when(even)
+        def _():
+            own[k].start()
+
+        @pl.when(jnp.logical_not(even))
+        def _():
+            passed[k].start()
+
+    halo[1].start()
     gain, shift = vectors[0:1, :], vectors[1:2, :]
     own_rows = pl.ds(2 * rows, rows)
-    first = (normed * gain + shift).astype(BF)
+    first = (norm_rows(tok[...]) * gain + shift).astype(BF)
     first_all[own_rows, :] = first
     first_t[:, own_rows] = first.T
-
+    pass_halo(0)
     arrive(segs)
     least = jnp.maximum(0, 2 * rows - b * rows)
     keys_doc = jnp.concatenate([seg_halo[0], seg_halo[1], seg[...]], 1).astype(F32)
@@ -371,20 +368,18 @@
         query_at = lax.broadcasted_iota(jnp.int32, (256, rows), 1) + 2 * rows
         allowed = (keys_doc[at, 0:1] == query_doc) & (key_at <= query_at) & (key_at >= least)
         bias[at, :] = jnp.where(allowed, 0.0, -1e30)
+    for t in range(3, n_chunks):
+        locals_[t].wait()
+    net.issue(5, 0)
     net.pass_on(0, 3)
-    net.pass_on(1, 3)
     net.pass_on(2, 3)
-    net.issue(5, 0)
-    for t in range(3):
-        net.done(t)
-    net.pass_on(3, 1)
+    net.issue(3, 0)
 
     def weight(first_col, width):
         value = g_att[:, :, :, pl.ds(first_col, width)]
         return value.reshape(D, width)
 
     scale = 1.0 / math.sqrt(HD)
-    do_s[...] = mm(grad[...], weight(3 * D, D), NT).astype(BF)
 
     def project(kind, j, at, out, factor):
         col = pl.multiple_of(kind * D + 256 * j, 256)
@@ -397,23 +392,42 @@
                 u = u * factor
             out[:, pl.ds(pl.multiple_of(256 * j + LANES * k, LANES), LANES)] = u.astype(BF)
 
-    def own_projections(j, carry):
+    def own_queries(j, carry):
         project(0, j, own_rows, q_s, scale)
+        return carry
+
+    def own_keys(j, carry):
         project(1, j, own_rows, k_s.at[own_rows], None)
+        return carry
+
+    def own_values(j, carry):
         project(2, j, own_rows, v_s.at[own_rows], None)
         return carry
 
-    lax.fori_loop(0, 3, own_projections, 0)
-    net.pass_on(4, 1)
+    net.done(0)
+    lax.fori_loop(0, 3, own_queries, 0)
+    lax.fori_loop(0, 1, own_keys, 0)
+    pass_halo(1)
+    net.pass_on(1, 3)
+    net.issue(4, 0)
+    net.done(2)
+    do_s[...] = mm(grad[...], weight(3 * D, D), NT).astype(BF)
+    lax.fori_loop(2, 3, own_values, 0)
+    net.pass_on(5, 1)
+    net.done(1)
+    lax.fori_loop(1, 3, own_keys, 0)
+    lax.fori_loop(0, 2, own_values, 0)
     own[0].wait_recv()
+    net.pass_on(3, 1)
+    net.issue(8, 0)
     own[1].wait_recv()
-    net.pass_on(5, 1)
     for k in range(2):
         at = slice(k * rows, (k + 1) * rows)
         before = (norm_rows(tok_halo[k]) * gain + shift).astype(BF)
         first_all[at, :] = before
         first_t[:, at] = before.T
-    net.pass_on(3, 2)
+    net.pass_on(4, 1)
+    net.pass_on(5, 2)
 
     def earlier_projections(j, carry):
         for k in range(2):
@@ -423,16 +437,23 @@
         return carry
 
     lax.fori_loop(0, 3, earlier_projections, 0)
+    net.pass_on(3, 2)
     net.issue(6, 0)
-    net.pass_on(4, 2)
-
+
+    go, send, end = net.pass_on, net.issue, net.done
     later = [
-        [lambda: net.pass_on(5, 2), lambda: net.issue(7, 0), lambda: net.pass_on(6, 1)],
-        [lambda: net.pass_on(3, 3), lambda: net.issue(8, 0)],
-        [lambda: net.pass_on(4, 3), lambda: net.pass_on(7, 1), lambda: net.pass_on(6, 2)],
-        [lambda: net.pass_on(5, 3), lambda: net.pass_on(8, 1), lambda: net.pass_on(7, 2)],
-        [lambda: net.pass_on(6, 3), lambda: net.pass_on(8, 2)],
-        [lambda: net.pass_on(7, 3)],
+        [(go, 8, 1), (send, 7, 0), (go, 4, 2)],
+        [(go, 5, 3)],
+        [(go, 6, 1)],
+        [(go, 3, 3), (go, 7, 1)],
+        [(go, 8, 2), (go, 6, 2)],
+        [(go, 4, 3), (go, 7, 2)],
+        [],
+        [(go, 8, 3)],
+        [],
+        [(go, 6, 3)],
+        [(go, 7, 3)],
+        [],
     ]
     tile = 256
 
@@ -493,19 +514,18 @@
             dq = jnp.concatenate(dqs, 0).T * scale
             at = slice(2 * rows + t * tile, 2 * rows + (t + 1) * tile)
             dq_s[cols, lanes] = rope(dq, cos_s[at, :], -low_s[at, :], -high_s[at, :]).astype(BF)
+            for k in range(PAIRS):
+
+                @pl.when(p == k)
+                def _(k=k, t=t):
+                    for event, *where in later[2 * k + t]:
+                        event(*where)
+
         dk_s[:, lanes] = rope(dk_acc[...], cos_s[...], -low_s[...], -high_s[...]).astype(BF)
         dv_s[:, lanes] = dv_acc[...].astype(BF)
-        for k, events in enumerate(later):
-
-            @pl.when(p == k)
-            def _(events=events):
-                for event in events:
-                    event()
-
         return carry
 
     lax.fori_loop(0, PAIRS, pair, 0)
-    net.pass_on(8, 3)
 
     def earlier_grad(k, carry):
         at = pl.ds(pl.multiple_of(k * 256, 256), 256)
@@ -754,20 +774,40 @@
     )
     for t in range(3):
         net.step(t, 0)
+    net.step(0, 1)
+    net.step(1, 1)
+    net.step(2, 1)
     even = lax.rem(b, 2) == 0
-    one, two = fg_prev.at[pl.ds(rows, rows)], fg_prev.at[pl.ds(0, rows)]
-    to_next = remote(one, hop, h_s.at[0], h_r.at[0], around[2])
-    to_last = remote(one, hop, h_s.at[0], h_r.at[0], around[3])
-    to_owner = remote(two, home, h_s.at[1], h_r.at[1], around[1])
-
-    @pl.when(even)
-    def _():
-        to_next.start()
-        to_owner.start()
-
-    @pl.when(jnp.logical_not(even))
-    def _():
-        to_last.start()
+    quarter = rows // 4
+    to_next, to_last, to_owner = [], [], []
+    for k in range(4):
+        near = fg_prev.at[pl.ds(rows + k * quarter, quarter)]
+        far = fg_prev.at[pl.ds(k * quarter, quarter)]
+        part = pl.ds(k * quarter, quarter)
+        to_next.append(remote(near, hop.at[part], h_s.at[k], h_r.at[k], around[2]))
+        to_last.append(remote(near, hop.at[part], h_s.at[k], h_r.at[k], around[3]))
+        to_owner.append(remote(far, home.at[part], h_s.at[4 + k], h_r.at[4 + k], around[1]))
+
+    def hop_halo(k):
+        @pl.when(even)
+        def _():
+            to_next[k].start()
+
+        @pl.when(jnp.logical_not(even))
+        def _():
+            to_last[k].start()
+
+    def forward_halo(k):
+        to_last[k].wait_recv()
+        at = pl.ds(k * quarter, quarter)
+
+        @pl.when(jnp.logical_not(even))
+        def _():
+            fg_prev[at, :] = (fg_prev[at, :].astype(F32) + hop[at, :].astype(F32)).astype(BF)
+
+        to_owner[k].start()
+
+    hop_halo(0)
 
     gain_first, gain_second = vectors[0:1, :], vectors[2:3, :]
     normed, factor = norm_parts(tok[...].astype(F32))
@@ -780,25 +820,20 @@
     sg_acc[...] = jnp.zeros_like(sg_acc)
     mine = v_c.at[c]
     mine[...] = jnp.zeros((16, D), F32)
-    net.step(0, 1)
-    net.step(1, 1)
-
+
+    step = net.step
     events = [
-        [(2, 1)],
-        [(3, 0), (0, 2)],
-        [(4, 0), (3, 1), (2, 2), (0, 3)],
-        [(4, 1), (1, 2), (5, 0)],
+        [(hop_halo, 1)],
+        [],
+        [(step, 2, 2)],
+        [(step, 3, 0), (step, 0, 2)],
+        [(step, 3, 1), (forward_halo, 0), (hop_halo, 2)],
+        [(step, 4, 0), (step, 1, 2)],
+        [(step, 4, 1), (forward_halo, 1), (hop_halo, 3), (step, 2, 3)],
+        [(step, 5, 0), (step, 6, 0), (step, 7, 0), (step, 8, 0), (step, 0, 3)],
     ]
     root = math.sqrt(0.5)
     level = 1.0 / math.sqrt(2.0 * math.pi)
-
-    def forward_halo():
-        to_last.wait_recv()
-
-        @pl.when(jnp.logical_not(even))
-        def _():
-            add_into(two.reshape((2, rows // 2, D)), [hop.reshape((2, rows // 2, D))])
-            to_owner.start()
 
     def chunk(k, squares):
         slot = lax.rem(k, 2)
@@ -824,6 +859,18 @@
             wide = act.astype(F32)
             squares = squares + jnp.sum(wide * wide, -1, keepdims=True)
             v_c[c, pl.ds(8 + k, 1), tile] = jnp.sum(pg.astype(F32), 0, keepdims=True)
+
+        def hook(half):
+            for n in range(FF_CHUNKS):
+
+                @pl.when(k == n)
+                def _(n=n):
+                    if half == 1 and n + 2 < FF_CHUNKS:
+                        start(loads[n + 2])
+                    for event, *where in events[2 * n + half]:
+                        event(*where)
+
+        hook(0)
         p_up[:, :, :, pl.ds(pl.multiple_of(D * k, 256), D)] = (
             mm(second_t[...], pg_s[...]).astype(BF).reshape(lay.nz, lay.ny, r, D)
         )
@@ -832,58 +879,61 @@
         )
         output_base[...] += mm(act_s[...], down)
         sg_acc[...] += mm(pg_s[...], w_up[slot].reshape(D, D), NT)
-        for n in range(FF_CHUNKS):
-
-            @pl.when(k == n)
-            def _(n=n):
-                if n + 2 < FF_CHUNKS:
-                    start(loads[n + 2])
-                for event in events[n]:
-                    net.step(*event)
-                if n == 2:
-                    forward_halo()
-
+        hook(1)
         return squares
 
     squares = lax.fori_loop(0, FF_CHUNKS, chunk, jnp.zeros((rows, 1), F32))
-    for t in (7, 8, 6):
-        net.step(t, 0)
+    run = lambda *pairs: [step(t, k) for t, k in pairs]
+    run((5, 1), (6, 1), (3, 2))
     output[...] = output_base[...].astype(BF)
-    for t, k in ((3, 2), (0, 4), (1, 3), (5, 1), (7, 1), (8, 1), (6, 1), (2, 3)):
-        net.step(t, k)
-
-    to_owner.wait_recv()
-    total_first = fg_own[...] + home[...].astype(F32)
-    keep = jnp.where(even, 1.0, 0.0).astype(F32)
-    fg_own[...] = total_first + hop[...].astype(F32) * keep
-    first_grad = fg_own[...]
-    second_grad = sg_acc[...]
-    normed, factor = norm_parts(tok[...].astype(F32))
-    input_grad[...] = (
-        grad[...].astype(F32)
-        + norm_back(first_grad, gain_first, normed, factor)
-        + norm_back(second_grad, gain_second, normed, factor)
-    ).astype(BF)
-    for t, k in ((3, 3), (1, 4), (4, 2), (2, 4), (0, 5)):
-        net.step(t, k)
+    forward_halo(2)
+    run((1, 3), (8, 1), (7, 1), (2, 4))
+    cot_sum = jnp.sum(grad[...].astype(F32), 0, keepdims=True)
+    run((0, 4))
+    forward_halo(3)
 
     def put(k, value):
         v_c[c, k : k + 1, :] = value
 
-    put(0, jnp.sum(first_grad * normed, 0, keepdims=True))
-    put(1, jnp.sum(first_grad, 0, keepdims=True))
-    put(2, jnp.sum(second_grad * normed, 0, keepdims=True))
-    put(3, jnp.sum(second_grad, 0, keepdims=True))
-    cot = grad[...].astype(F32)
-    put(4, jnp.sum(cot, 0, keepdims=True))
+    put(4, cot_sum)
     for k in range(3):
         put(5 + k, att_sums[k : k + 1, :])
+    cot = grad[...].astype(F32)
     token_norm = squares * jnp.sum(cot * cot, -1, keepdims=True) * (1.0 / (FF * D))
     docs_of = jnp.concatenate([seg[...].astype(F32)] * (LANES // 8), 0).T[:, 0:1]
     doc = lax.broadcasted_iota(jnp.int32, (rows, D), 1).astype(F32)
     member = jnp.where((docs_of == doc) & (doc < docs), 1.0, 0.0)
     put(12, jnp.sum(token_norm * member, 0, keepdims=True))
     put(13, jnp.sum(member, 0, keepdims=True))
+    run((4, 2))
+    keep = jnp.where(even, 1.0, 0.0).astype(F32)
+
+    def norms(k):
+        to_owner[k].wait_recv()
+        at = slice(k * quarter, (k + 1) * quarter)
+        first_grad = fg_own[at, :] + home[at, :].astype(F32) + hop[at, :].astype(F32) * keep
+        second_grad = sg_acc[at, :]
+        normed, factor = norm_parts(tok[at, :].astype(F32))
+        input_grad[at, :] = (
+            grad[at, :].astype(F32)
+            + norm_back(first_grad, gain_first, normed, factor)
+            + norm_back(second_grad, gain_second, normed, factor)
+        ).astype(BF)
+        sums = [first_grad * normed, first_grad, second_grad * normed, second_grad]
+        return [jnp.sum(value, 0, keepdims=True) for value in sums]
+
+    def add_up(left, right):
+        return [p + q for p, q in zip(left, right)]
+
+    sums = norms(0)
+    run((5, 2), (1, 4))
+    sums = add_up(sums, norms(1))
+    run((6, 2), (3, 3))
+    sums = add_up(sums, norms(2))
+    sums = add_up(sums, norms(3))
+    for k in range(4):
+        put(k, sums[k])
+    run((8, 2))
 
     at = [0, 1, lay.nx, lay.nx + lay.ny - 1]
 
@@ -905,33 +955,27 @@
         return value
 
     start(vec_c)
-    net.step(5, 2)
-    net.step(3, 4)
+    run((7, 2), (4, 3))
     arrive(vec_c)
     v_x[x] = add_all(v_c, 2)
     start(vec_x)
-    for t, k in ((7, 2), (8, 2), (4, 3), (6, 2), (1, 5), (2, 5)):
-        net.step(t, k)
+    run((2, 5), (0, 5), (3, 4), (6, 3), (5, 3))
     arrive(vec_x)
     v_y[y] = add_all(v_x, lay.nx)
     start(vec_y)
-    for t, k in ((7, 3), (4, 4), (5, 3)):
-        net.step(t, k)
+    run((1, 5), (8, 3), (4, 4), (3, 5), (7, 3))
     arrive(vec_y)
     v_z[z] = add_all(v_y, lay.ny)
     start(vec_z)
-    for t, k in ((6, 3), (3, 5), (7, 4), (8, 3), (4, 5), (5, 4)):
-        net.step(t, k)
+    run((6, 4), (5, 4), (4, 5), (8, 4), (6, 5), (5, 5), (7, 4), (8, 5))
     arrive(vec_z)
     vec_out[...] = add_all(v_z, lay.nz)
-    for t, k in ((7, 5), (5, 5), (6, 4), (8, 4), (6, 5), (8, 5)):
-        net.step(t, k)
+    run((7, 5))
     for t in range(9):
         net.step(t, 6)
     net.drain()
     sent(vec_c + vec_x + vec_y + vec_z)
-    to_next.wait_send()
-    to_owner.wait_send()
+    sent(to_next + to_owner)
 
 
 def back(lay, g_up, g_down, p_att, fg_prev, fg_own, attn_out, vectors, up_add, att_sums, tok, grad, seg):
@@ -971,7 +1015,7 @@
     nv = 1 + lay.nx + lay.ny + lay.nz
     sems = [
         dma(n), dma(n), dma(n, lx), dma(n, lx), dma(n, ly), dma(n, ly), dma(n, lz), dma(n, lz),
-        dma(n, lx), dma(n, lx), dma(n), dma(n), dma(nv), dma(nv), dma(2, FF_CHUNKS), dma(2), dma(2),
+        dma(n, lx), dma(n, lx), dma(n), dma(n), dma(nv), dma(nv), dma(2, FF_CHUNKS), dma(8), dma(8),
     ]
     vmem = pl.BlockSpec(memory_space=pltpu.VMEM)
     return pl.pallas_call(

time: 289 us -> 253 us (0.88)
  Pallas kernels: 265 us -> 231 us
    pallas_call x1, Pallas kernels: 122 us -> 104 us  [back(): pl.pallas_call(functools.partial(back_kernel, lay, rows, docs), name='bac...]
    pallas_call x1, Pallas kernels: 143 us -> 127 us  [front(): pl.pallas_call(functools.partial(front_kernel, lay, rows), name='front',...]
where the time goes in v2:
time: 253 us; the launch traced here: 252 us
  Pallas kernels  231 us (91%)
  local copies, waits for them, and re-layouts  13 us (5%)
  other arithmetic  7.77 us (3%)
    pallas_call x1, Pallas kernels, front(): pl.pallas_call(functools.partial(front_kernel, lay, rows), name='front',...  127 us
    pallas_call x1, Pallas kernels, back(): pl.pallas_call(functools.partial(back_kernel, lay, rows, docs), name='bac...  104 us
    unnamed x28, local copies, waits for them, and re-layouts  5.25 us

profile of v2, /device:TPU:1, one launch (start us, length us, event | category | flops | bytes accessed | tf_op | source)
XLA Modules:
  0.0 252.4 jit_solution(7777283056456699380)
XLA Ops:
  0.6 1.3 broadcast_in_dim.2.seg
  1.9 1.3 copy.30
  3.3 0.0 copy-start.4
  3.3 0.0 copy-start.5
  3.3 0.0 copy-start.7
  3.4 0.0 copy-start.9
  3.4 0.0 copy-start.10
  3.4 0.0 copy-start.6
  3.4 0.2 copy.32
  3.6 0.5 copy-done.4
  4.2 0.9 pad_maximum_fusion.u_att
  5.0 0.1 tile.75
  5.1 0.1 tile.77
  5.2 0.1 tile.60
  5.3 0.1 tile.62
  5.4 0.1 tile.63
  5.5 0.1 tile.65
  5.6 0.1 tile.66
  5.7 0.1 tile.68
  5.8 0.1 tile.69
  5.9 0.1 tile.71
  6.0 0.1 tile.72
  6.1 0.1 tile.74
  6.1 0.3 concatenate.7
  6.4 0.6 pad_convert_fusion.small
  7.1 126.8 %front.1 = (bf16[4,2,96,3072]{3,2,1,0:T(8,128)(2,1)}, bf16[4,2,4,96,768]{4,3,2,1,0:T(8,128)(2,1)}, bf16[4,2,96,3072]{3,2,1,0:T(8,128)(2,1)}, bf16[1024,768]{1,0:...) custom-call(bf16[96,3072]{1,0:T(8,128)(2,1)} %pad_maximum_fusion.u_a, ...), custom_call_target="tpu_custom_call" | custom-call | tf_op jit(solution)/shard_map/front/pallas_call | solution.py:594
  133.8 104.0 %back.1 = (bf16[512,768]{1,0:T(8,128)(2,1)}, bf16[512,768]{1,0:T(8,128)(2,1)}, bf16[96,3072]{1,0:T(8,128)(2,1)}, bf16[96,3072]{1,0:T(8,128)(2,1)}, bf16[4,96,768]{2,1,0:T(8,128)(2,1)}, /*index=5*/f32[16,768]{1,0:T(8,128)}) custom-call(bf16[4,2,96,3072]{3,2,1,0:T(8,128)(2,1)} %get-tuple-element.29.g_up, bf16[4,2,4,96,768]{4,3,2,1,0:T(8,128)(2,1)} %get-tuple-element.30.g_down, ...), custom_call_target="tpu_custom_call" | custom-call | tf_op jit(solution)/shard_map/back/pallas_call | solution.py:1021
  237.9 0.7 slice.36
  238.6 0.1 constant_dynamic-slice_fusion
  238.7 0.5 slice_bitcast_fusion
  239.2 0.7 slice.42
  240.0 0.1 reshape.91
  240.1 0.1 reshape.92
  240.2 0.7 dynamic_slice.10
  240.8 0.7 slice.44
  241.6 0.7 dynamic_slice.11
  242.2 1.3 fusion
  243.5 1.1 slice_convert_fusion
  244.6 0.4 copy.33
  244.9 0.1 copy.34
  245.1 1.3 copy.36
  246.3 1.7 slice_convert_fusion.1
  248.1 1.1 bitcast_convert_fusion
  249.2 1.1 convert_element_type.17
  250.3 0.3 copy-done.1
  250.6 0.9 copy.41
  251.5 0.0 copy-done
  251.5 0.9 copy.42
  (24 shorter events, 0.1 us)
Async XLA Ops:
  3.3 0.9 copy-start.4
  3.3 1.7 copy-start.5
  3.3 1.9 copy-start.7
  3.3 2.1 copy-start.8
  3.4 2.2 copy-start.9
  3.4 2.4 copy-start.10
  3.4 2.6 %copy-start.11 = (bf16[96]{0:T(256)(128)(2,1)S(1)}, bf16[96]{0:T(256)(128)(2,1)}, u32[]{:S(2)}) copy-start(bf16[96]{0:T(256)(128)(2,1)} %param.27) | copy-start | bytes 580
  3.4 2.8 %copy-start.6 = (bf16[384]{0:T(512)(128)(2,1)S(1)}, bf16[384]{0:T(512)(128)(2,1)}, u32[]{:S(2)}) copy-start(bf16[384]{0:T(512)(128)(2,1)} %param.25) | copy-start | bytes 2308
  245.1 3.0 %copy-start.3 = (bf16[4,96,768]{2,1,0:T(8,128)(2,1)S(1)}, bf16[4,96,768]{2,1,0:T(8,128)(2,1)}, u32[]{:S(2)}) copy-start(bf16[4,96,768]{2,1,0:T(8,128)(2,1)} %get-tuple-element.43) | copy-start | bytes 1769476
  246.3 2.8 %copy-start.2 = (bf16[96,3072]{1,0:T(8,128)(2,1)S(1)}, bf16[96,3072]{1,0:T(8,128)(2,1)}, u32[]{:S(2)}) copy-start(bf16[96,3072]{1,0:T(8,128)(2,1)} %get-tuple-element.42) | copy-start | bytes 1769476
  249.2 1.4 copy-start.1
  250.3 1.2 copy-start

commit v3 on v2

--- a/solution.py
+++ b/solution.py
@@ -153,19 +153,12 @@
 def small_plan(r):
     plan, at = [], 0
     for size, within in [(r, LANES)] * 5 + [(3 * r, HD), (4 * r, LANES)]:
-        unit = math.gcd(size, within)
-        plan.append((at, size // unit, unit))
-        at += size // unit
+        plan.append((at, size, math.gcd(size, within)))
+        at += -(-size // LANES)
     return plan
 
 
-def pack_small(vectors, r):
-    rows = [
-        jnp.tile(v.reshape(-1, unit), (1, LANES // unit))
-        for v, (_, _, unit) in zip(vectors, small_plan(r))
-    ]
-    packed = jnp.concatenate(rows, 0).astype(F32)
-    return jnp.pad(packed, ((0, -packed.shape[0] % 8), (0, 0)))
+SMALL_ROWS = 16
 
 
 class Gather:
@@ -216,18 +209,35 @@
 
 def front_kernel(
     lay, rows,
-    u_att, u_up, u_down, small, tok, grad, seg,
-    g_up, g_down, p_att, fg_prev, fg_own, attn_out, vectors, up_add, att_sums,
-    g_att, g_small, tok_halo, seg_halo, first_all, first_t, q_s, k_s, v_s, do_s, ctx_s, ctx_t,
+    u_up, u_down, qkv, dense, tok, grad, seg, v0, v1, v2, v3, v4, v5, v6,
+    g_up, g_down, p_out, prev_out, own_out, attn_hbm, vectors, up_add, att_sums,
+    small, u_att, p_att, fg_prev, fg_own, attn_out, g_att, g_small, tok_halo, seg_halo, first_all, first_t, q_s, k_s, v_s, do_s, ctx_s, ctx_t,
     dq_s, dk_s, dv_s, cos_s, low_s, high_s, bias, dk_acc, dv_acc, qkv_add, s_s, w_s, d_s,
-    local_sem, z_s, z_r, y_s, y_r, x_s, x_r, c_s, c_r, sm_s, sm_r, h_s, h_r,
+    local_sem, z_s, z_r, y_s, y_r, x_s, x_r, c_s, c_r, sm_s, sm_r, h_s, h_r, out_sem,
 ):
     span = 3 * rows
-    r = u_att.shape[0]
+    r = qkv.shape[0]
     n_chunks = len(CHUNKS)
     x, c, z, y = lay.coords()
     xs, cs, zs, ys = line_peers(lay)
     total = lay.dp * lay.fsdp
+    plan = small_plan(r)
+    for (row, size, _), ref in zip(plan, (v0, v1, v2, v3, v4, v5, v6)):
+        value = ref[...].astype(F32).reshape(1, size)
+        for k in range(-(-size // LANES)):
+            width = min(LANES, size - k * LANES)
+            small[row + k : row + k + 1, :width] = value[:, k * LANES : k * LANES + width]
+    left = lax.broadcasted_iota(jnp.int32, (r, LANES), 1) < HD
+    for p in range(PAIRS):
+        parts = [qkv[:, (3 * p + k) * LANES : (3 * p + k + 1) * LANES].astype(F32) for k in range(3)]
+        kinds = (
+            jnp.where(left, parts[0], parts[1]),
+            pltpu.roll(jnp.where(left, parts[2], parts[0]), HD, 1),
+            jnp.where(left, parts[1], parts[2]),
+        )
+        for k, part in enumerate(kinds):
+            u_att[:, k * D + p * LANES : k * D + (p + 1) * LANES] = part.astype(BF)
+    u_att[:, 3 * D :] = dense[...]
     b = lax.axis_index("dp") * lay.fsdp + lax.axis_index("fsdp")
 
     def stream(k):
@@ -306,15 +316,17 @@
 
     lane_row = lax.broadcasted_iota(jnp.int32, (1, LANES), 1)
 
-    def line(first_row, per, unit, length, source):
+    def line(first_row, size, unit, length, source):
         out = []
         for block in range(length // LANES):
             value = None
             for k in range(LANES // unit):
-                at = source(block * (LANES // unit) + k)
-                owner = at // per
-                row = first_row + at % per
+                owner, local = divmod(source(block * (LANES // unit) + k), size // unit)
+                row, lane = divmod(local * unit, LANES)
+                row += first_row
                 piece = g_small[owner // lay.ny, owner % lay.ny, row : row + 1, :]
+                if lane != k * unit:
+                    piece = pltpu.roll(piece, (k * unit - lane) % LANES, 1)
                 value = piece if value is None else jnp.where(lane_row // unit == k, piece, value)
             out.append(value)
         return jnp.concatenate(out, 1)
@@ -322,7 +334,6 @@
     def norm_rows(values):
         return norm_parts(values.astype(F32))[0]
 
-    plan = small_plan(r)
     for j in range(5):
         vectors[j : j + 1, :] = line(*plan[j], D, lambda n: n)
     vectors[5:8, :] = jnp.zeros((3, D), F32)
@@ -359,7 +370,7 @@
     arrive(segs)
     least = jnp.maximum(0, 2 * rows - b * rows)
     keys_doc = jnp.concatenate([seg_halo[0], seg_halo[1], seg[...]], 1).astype(F32)
-    keys_doc = jnp.concatenate([keys_doc] * (LANES // 8), 0).T
+    keys_doc = jnp.broadcast_to(keys_doc, (LANES, span)).T
     query_doc = seg[0:1, :].astype(F32)
 
     for k in range(6):
@@ -534,6 +545,8 @@
         return carry
 
     lax.fori_loop(0, 2 * rows // 256, earlier_grad, 0)
+    outs = [pltpu.make_async_copy(fg_prev, prev_out, out_sem.at[0])]
+    outs[0].start()
     for k in range(rows // 256):
         at = slice(2 * rows + 256 * k, 2 * rows + 256 * (k + 1))
         near = slice(256 * k, 256 * (k + 1))
@@ -543,6 +556,9 @@
             + mm(dq_s[near, :], weight(0, D), NT)
         )
 
+    outs.append(pltpu.make_async_copy(fg_own, own_out, out_sem.at[1]))
+    outs[1].start()
+
     def weight_grads(j, carry):
         col = pl.multiple_of(256 * j, 256)
         cols = pl.ds(col, 256)
@@ -560,6 +576,9 @@
         return carry
 
     lax.fori_loop(0, 3, weight_grads, 0)
+    outs.append(pltpu.make_async_copy(p_att, p_out, out_sem.at[2]))
+    outs.append(pltpu.make_async_copy(attn_out, attn_hbm, out_sem.at[3]))
+    start(outs[2:])
     for k, ref in enumerate((dq_s, dk_s, dv_s)):
         att_sums[k : k + 1, :] = jnp.sum(ref[...].astype(F32), 0, keepdims=True)
     att_sums[3:8, :] = jnp.zeros((5, D), F32)
@@ -567,12 +586,14 @@
         net.done(t)
     net.drain()
     sent(small_z + small_y + segs + halo + own)
-
-
-def front(lay, u_att, u_up, u_down, small, tok, grad, seg):
+    for copy in outs:
+        copy.wait()
+
+
+def front(lay, u_up, u_down, qkv, dense, tok, grad, seg, vectors):
     rows = tok.shape[0]
     span = 3 * rows
-    r = u_att.shape[0]
+    r = qkv.shape[0]
     n = len(CHUNKS)
     outs = (
         jax.ShapeDtypeStruct(grad_shape(lay, 1, r), BF),
@@ -595,22 +616,23 @@
         functools.partial(front_kernel, lay, rows),
         name="front",
         out_shape=outs,
-        in_specs=hbm(3) + [vmem] * 4,
-        out_specs=tuple(hbm(2)) + (vmem,) * 7,
+        in_specs=hbm(2) + [vmem] * (5 + len(vectors)),
+        out_specs=tuple(hbm(6)) + (vmem,) * 3,
         scratch_shapes=[
-            v(grad_shape(lay, 0, r)), v((lay.nz, lay.ny) + small.shape, F32), v((2, rows, D)),
-            v((2, 8, rows), jnp.int32), v((span, D)), v((D, span)), v((rows, D)), v((span, D)),
+            v((SMALL_ROWS, LANES), F32), v((r, 4 * D)), v(grad_shape(lay, 0, r)), v((2 * rows, D)), v((rows, D), F32), v((rows, D), F32),
+            v(grad_shape(lay, 0, r)), v((lay.nz, lay.ny, SMALL_ROWS, LANES), F32), v((2, rows, D)),
+            v((2, 1, rows), jnp.int32), v((span, D)), v((D, span)), v((rows, D)), v((span, D)),
             v((span, D)), v((rows, D)), v((rows, D)), v((D, rows)), v((rows, D)), v((span, D)),
             v((span, D)), v((span, LANES), F32), v((span, LANES), F32), v((span, LANES), F32),
             v((span, rows), F32), v((span, LANES), F32), v((span, LANES), F32), v((1, 3 * D), F32),
             v((2, span, 256), F32), v((2, span, 256)), v((2, span, 256)),
             dma(n + 1), dma(n, lz), dma(n, lz), dma(n, ly), dma(n, ly), dma(n, lx), dma(n, lx),
-            dma(n), dma(n), dma(lay.nz + ly), dma(lay.nz + ly), dma(6), dma(6),
+            dma(n), dma(n), dma(lay.nz + ly), dma(lay.nz + ly), dma(6), dma(6), dma(4),
         ],
         compiler_params=pltpu.CompilerParams(
             collective_id=0, has_side_effects=True, vmem_limit_bytes=VMEM_LIMIT
         ),
-    )(u_att, u_up, u_down, small, tok, grad, seg)
+    )(u_up, u_down, qkv, dense, tok, grad, seg, *vectors)
 
 
 class Reduce:
@@ -735,13 +757,13 @@
 
 def back_kernel(
     lay, rows, docs,
-    g_up, g_down, p_att, fg_prev, fg_own, attn_out, vectors, up_add, att_sums, tok, grad, seg,
+    g_up, g_down, p_in, prev_in, own_in, attn_in, vectors, up_add, att_sums, tok, grad, seg,
     output, input_grad, f_att, f_up, f_down, vec_out,
-    p_up, p_down, w_up, w_down, second_in, second_t, act_s, pg_s, sg_acc, hop, home,
+    p_att, fg_prev, fg_own, attn_out, p_up, p_down, w_up, w_down, second_in, second_t, act_s, pg_s, sg_acc, hop, home,
     ca, ra1, rb1, ra2, rb2, ra3, v_c, v_x, v_y, v_z, *sems,
 ):
-    (c_s, c_r, x_s, x_r, y_s, y_r, z_s, z_r, fx_s, fx_r, fc_s, fc_r, v_s, v_r, w_sem, h_s, h_r) = sems
-    r = p_att.shape[2]
+    (c_s, c_r, x_s, x_r, y_s, y_r, z_s, z_r, fx_s, fx_r, fc_s, fc_r, v_s, v_r, w_sem, h_s, h_r, in_sem) = sems
+    r = p_in.shape[2]
     x, c, z, y = lay.coords()
     xs, cs, zs, ys = line_peers(lay)
     total = lay.dp * lay.fsdp
@@ -766,17 +788,31 @@
                 ),
             )
         )
+    taken = [
+        pltpu.make_async_copy(
+            p_in.at[:, :, :, pl.ds(1024 * i, 1024)], p_att.at[:, :, :, pl.ds(1024 * i, 1024)],
+            in_sem.at[i],
+        )
+        for i in range(3)
+    ]
+    taken.append(pltpu.make_async_copy(prev_in, fg_prev, in_sem.at[3]))
+    taken.append(pltpu.make_async_copy(attn_in, attn_out, in_sem.at[4]))
+    taken.append(pltpu.make_async_copy(own_in, fg_own, in_sem.at[5]))
+    start(taken[:4])
     start(loads[0])
+    start(taken[4:])
     start(loads[1])
     barrier_with(xs + cs + zs + ys + around)
     net = Reduce(
         lay, (p_att, p_up, p_down), (f_att, f_up, f_down), (ca, ra1, rb1, ra2, rb2, ra3), sems[:12]
     )
     for t in range(3):
+        taken[t].wait()
         net.step(t, 0)
     net.step(0, 1)
     net.step(1, 1)
     net.step(2, 1)
+    taken[3].wait()
     even = lax.rem(b, 2) == 0
     quarter = rows // 4
     to_next, to_last, to_owner = [], [], []
@@ -815,6 +851,8 @@
     second_in[...] = value
     second_t[...] = value.T
     cot = grad[...].astype(F32)
+    taken[4].wait()
+    taken[5].wait()
     output_base = attn_out
     output_base[...] = attn_out[...] + tok[...].astype(F32) + vectors[4:5, :]
     sg_acc[...] = jnp.zeros_like(sg_acc)
@@ -900,7 +938,7 @@
         put(5 + k, att_sums[k : k + 1, :])
     cot = grad[...].astype(F32)
     token_norm = squares * jnp.sum(cot * cot, -1, keepdims=True) * (1.0 / (FF * D))
-    docs_of = jnp.concatenate([seg[...].astype(F32)] * (LANES // 8), 0).T[:, 0:1]
+    docs_of = jnp.broadcast_to(seg[...].astype(F32), (LANES, rows)).T[:, 0:1]
     doc = lax.broadcasted_iota(jnp.int32, (rows, D), 1).astype(F32)
     member = jnp.where((docs_of == doc) & (doc < docs), 1.0, 0.0)
     put(12, jnp.sum(token_norm * member, 0, keepdims=True))
@@ -1000,6 +1038,7 @@
         return [v((chunks,) + peers + part_shape(lay, g, x_all, z_all, y_all, r)) for g in range(3)]
 
     scratch = [
+        v(grad_shape(lay, 0, r)), v((2 * rows, D)), v((rows, D), F32), v((rows, D), F32),
         v(grad_shape(lay, 1, r)), v(grad_shape(lay, 2, r)),
         v((2, lay.nz, lay.ny, r, D)), v((2, lay.nz // FF_CHUNKS, lay.ny, 4, r, D)),
         v((rows, D)), v((D, rows)), v((rows, D)), v((rows, D)), v((rows, D), F32),
@@ -1015,14 +1054,14 @@
     nv = 1 + lay.nx + lay.ny + lay.nz
     sems = [
         dma(n), dma(n), dma(n, lx), dma(n, lx), dma(n, ly), dma(n, ly), dma(n, lz), dma(n, lz),
-        dma(n, lx), dma(n, lx), dma(n), dma(n), dma(nv), dma(nv), dma(2, FF_CHUNKS), dma(8), dma(8),
+        dma(n, lx), dma(n, lx), dma(n), dma(n), dma(nv), dma(nv), dma(2, FF_CHUNKS), dma(8), dma(8), dma(6),
     ]
     vmem = pl.BlockSpec(memory_space=pltpu.VMEM)
     return pl.pallas_call(
         functools.partial(back_kernel, lay, rows, docs),
         name="back",
         out_shape=outs,
-        in_specs=hbm(2) + [vmem] * 10,
+        in_specs=hbm(6) + [vmem] * 6,
         out_specs=(vmem,) * 6,
         scratch_shapes=scratch + vecs + sems,
         compiler_params=pltpu.CompilerParams(
@@ -1031,45 +1070,83 @@
     )(g_up, g_down, p_att, fg_prev, fg_own, attn_out, vectors, up_add, att_sums, tok, grad, seg)
 
 
+def finish_kernel(
+    lay, docs, r, f_att, f_up, f_down, vec, out_in, grad_in,
+    output, input_grad, fg, fb, sg, sb, qkv_w, qkv_b, dense_w, up_w, up_b, down_w, ob, norms,
+):
+    output[...] = out_in[...]
+    input_grad[...] = grad_in[...]
+    shard = lax.axis_index("fsdp")
+
+    def by_head(row_count, kind):
+        left = lax.broadcasted_iota(jnp.int32, (row_count, LANES), 1) < HD
+        for p in range(PAIRS):
+            q, k, v = (kind(n, p) for n in range(3))
+            turned = pltpu.roll(k, HD, 1)
+            yield jnp.where(left, q, turned)
+            yield jnp.where(left, v, q)
+            yield jnp.where(left, turned, v)
+
+    def block(k, p):
+        return f_att[:, k * D + p * LANES : k * D + (p + 1) * LANES].astype(F32)
+
+    for n, value in enumerate(by_head(r, block)):
+        qkv_w[:, n * LANES : (n + 1) * LANES] = value
+    dense_w[...] = f_att[:, 3 * D :].astype(F32)
+    up_w[...] = f_up[...].astype(F32)
+    down_w[...] = f_down[...].astype(F32)
+
+    def own(row, width):
+        length = row.shape[1]
+        wide = jnp.broadcast_to(row, (8, length))
+        turned = pltpu.roll(wide, lax.rem(length - shard * width, length), 1)
+        return turned[0:1, :width].reshape(width)
+
+    for k, ref in enumerate((fg, fb, sg, sb, ob)):
+        ref[...] = own(vec[k : k + 1, :], r)
+    bias = list(by_head(1, lambda k, p: vec[5 + k : 6 + k, p * LANES : (p + 1) * LANES]))
+    qkv_b[...] = own(jnp.concatenate(bias, 1), 3 * r)
+    up_b[...] = own(jnp.concatenate([vec[8 + k : 9 + k, :] for k in range(4)], 1), 4 * r)
+    norms[...] = (vec[12:13, :docs] / vec[13:14, :docs]).reshape(docs)
+
+
+def finish(lay, output, input_grad, f_att, f_up, f_down, vec):
+    r = f_att.shape[0]
+    docs = DOC_DEV * lay.dp * lay.fsdp
+    vmem = pl.BlockSpec(memory_space=pltpu.VMEM)
+    shapes = [
+        (r,), (r,), (r,), (r,), (r, 3 * D), (3 * r,), (r, D), (r, FF), (4 * r,), (4, r, D), (r,), (docs,),
+    ]
+    return pl.pallas_call(
+        functools.partial(finish_kernel, lay, docs, r),
+        name="finish",
+        out_shape=tuple(jax.ShapeDtypeStruct(v.shape, v.dtype) for v in (output, input_grad))
+        + tuple(jax.ShapeDtypeStruct(shape, F32) for shape in shapes),
+        in_specs=[vmem] * 6,
+        out_specs=(vmem,) * (2 + len(shapes)),
+        compiler_params=pltpu.CompilerParams(vmem_limit_bytes=VMEM_LIMIT),
+    )(f_att, f_up, f_down, vec, output, input_grad)
+
+
 def per_device(
     lay, tokens, seg_ids, out_grad, first_gain, first_bias, second_gain, second_bias,
     qkv_weight, qkv_bias, dense_weight, up_weight, up_bias, down_weight, out_bias,
 ):
     rows = tokens.shape[0]
     r = qkv_weight.shape[0]
-    fsdp = lay.fsdp
-    qkv_kinds = qkv_weight.reshape(r, H, 3, HD).transpose(0, 2, 1, 3).reshape(r, 3 * D)
-    u_att = jnp.concatenate([qkv_kinds, dense_weight], 1)
-    u_down = down_weight.reshape(4, r, D)
     vectors = (first_gain, first_bias, second_gain, second_bias, out_bias, qkv_bias, up_bias)
-    small = pack_small(vectors, r)
-    seg_rows = jnp.broadcast_to(seg_ids[None, :], (8, rows))
-    passed = front(lay, u_att, up_weight, u_down, small, tokens, out_grad, seg_rows)
-    output, input_grad, f_att, f_up, f_down, vec = back(lay, *passed, tokens, out_grad, seg_rows)
-    docs = DOC_DEV * lay.dp * fsdp
-    shard = lax.axis_index("fsdp")
-    plain = lax.dynamic_slice_in_dim(vec[:5], shard * r, r, 1)
-    kinds = vec[5:8].reshape(3, H, HD).transpose(1, 0, 2).reshape(3 * D)
-    qkv_add = lax.dynamic_slice_in_dim(kinds, shard * 3 * r, 3 * r)
-    up_add = lax.dynamic_slice_in_dim(vec[8:12].reshape(FF), shard * 4 * r, 4 * r)
-    qkv_out = (
-        f_att[:, : 3 * D].astype(F32).reshape(r, 3, H, HD).transpose(0, 2, 1, 3).reshape(r, 3 * D)
+    seg_row = seg_ids.reshape(1, rows)
+    passed = front(
+        lay, up_weight, down_weight.reshape(4, r, D), qkv_weight, dense_weight, tokens,
+        out_grad, seg_row, vectors,
+    )
+    summed = back(lay, *passed, tokens, out_grad, seg_row)
+    (output, input_grad, fg, fb, sg, sb, qkv_w, qkv_b, dense_w, up_w, up_b, down_w, ob, norms) = finish(
+        lay, *summed
     )
     return (
-        output,
-        input_grad,
-        plain[0],
-        plain[1],
-        plain[2],
-        plain[3],
-        qkv_out,
-        qkv_add,
-        f_att[:, 3 * D :].astype(F32),
-        f_up.astype(F32),
-        up_add,
-        f_down.reshape(4 * r, D).astype(F32),
-        plain[4],
-        vec[12, :docs] / vec[13, :docs],
+        output, input_grad, fg, fb, sg, sb, qkv_w, qkv_b, dense_w, up_w, up_b,
+        down_w.reshape(4 * r, D), ob, norms,
     )
 
 

time: 253 us -> 232 us (0.917)
  local copies, waits for them, and re-layouts: 13 us -> 0 us
  other arithmetic: 7.77 us -> 0 us
    unnamed x28 -> x0, local copies, waits for them, and re-layouts: 5.25 us -> none
    pallas_call x0 -> x1, Pallas kernels: none -> 4.46 us  [finish(): pl.pallas_call(functools.partial(finish_kernel, lay, docs, r), name='fini...]
    convert_element_type x3 -> x0, other arithmetic: 3.95 us -> none  [the longest x1 1.7 us: per_device(): f_att[:, 3 * D:].astype(F32)]
    pallas_call x1, Pallas kernels: 104 us -> 101 us  [back(): pl.pallas_call(functools.partial(back_kernel, lay, rows, docs), name='bac...]
where the time goes in v3:
time: 232 us
  Pallas kernels  231 us (100%)
    pallas_call x1, Pallas kernels, front(): pl.pallas_call(functools.partial(front_kernel, lay, rows), name='front',...  125 us
    pallas_call x1, Pallas kernels, back(): pl.pallas_call(functools.partial(back_kernel, lay, rows, docs), name='bac...  101 us

profile of v3, /device:TPU:1, one launch (start us, length us, event | category | flops | bytes accessed | tf_op | source)
XLA Modules:
  0.0 231.6 jit_solution(8689230259007760468)
XLA Ops:
  0.6 125.2 %front.1 = (bf16[4,2,96,3072]{3,2,1,0:T(8,128)(2,1)}, bf16[4,2,4,96,768]{4,3,2,1,0:T(8,128)(2,1)}, bf16[4,2,96,3072]{3,2,1,0:T(8,128)(2,1)}, bf16[1024,768]{1,0:...) custom-call(bf16[96,3072]{1,0:T(8,128)(2,1)} %u_up.1, ...), custom_call_target="tpu_custom_call" | custom-call | tf_op jit(solution)/shard_map/front/pallas_call | solution.py:615
  125.8 101.1 %back.1 = (bf16[512,768]{1,0:T(8,128)(2,1)}, bf16[512,768]{1,0:T(8,128)(2,1)}, bf16[96,3072]{1,0:T(8,128)(2,1)}, bf16[96,3072]{1,0:T(8,128)(2,1)}, bf16[4,96,768]{2,1,0:T(8,128)(2,1)}, /*index=5*/f32[16,768]{1,0:T(8,128)}) custom-call(bf16[4,2,96,3072]{3,2,1,0:T(8,128)(2,1)} %get-tuple-element.43.g_up, bf16[4,2,4,96,768]{4,3,2,1,0:T(8,128)(2,1)} %get-tuple-element.44.g_down, ...), custom_call_target="tpu_custom_call" | custom-call | tf_op jit(solution)/shard_map/back/pallas_call | solution.py:1060
  226.9 4.5 %finish.1 = (bf16[512,768]{1,0:T(8,128)(2,1)}, bf16[512,768]{1,0:T(8,128)(2,1)}, f32[96]{0:T(128)}, f32[96]{0:T(128)}, f32[96]{0:T(128)}, /*index=5*/f32[96]{0:T...) custom-call(bf16[96,3072]{1,0:T(8,128)(2,1)} %get-tuple-element.52.f, ...), custom_call_target="tpu_custom_call" | custom-call | tf_op jit(solution)/shard_map/finish/pallas_call | solution.py:1120

commit v4 on v3

--- a/solution.py
+++ b/solution.py
@@ -135,6 +135,7 @@
 
 NT = (((1,), (1,)), ((), ()))
 NN = (((1,), (0,)), ((), ()))
+TN = (((0,), (0,)), ((), ()))
 F32 = jnp.float32
 BF = jnp.bfloat16
 
@@ -203,6 +204,110 @@
                 sent(copies)
 
 
+class Reduce:
+    def __init__(self, lay, ps, fs, bufs, sems, wanted):
+        (ca, ra1, rb1, ra2, rb2, ra3) = bufs
+        (c_s, c_r, x_s, x_r, y_s, y_r, z_s, z_r, fx_s, fx_r, fc_s, fc_r) = sems
+        x, c, z, y = lay.coords()
+        xs, cs, zs, ys = line_peers(lay)
+        other_x = [wrap(x + 1 + k, lay.nx) for k in range(lay.nx - 1)]
+        other_y = [wrap(y + 1 + k, lay.ny) for k in range(lay.ny - 1)]
+        other_z = [wrap(z + 1 + k, lay.nz) for k in range(lay.nz - 1)]
+        self.copies, self.adds = {}, {}
+        for t, stages in wanted.items():
+            g, i = CHUNKS[t]
+            p = ps[g]
+
+            def along(pieces, slot, peers, ss, rs, t=t):
+                return [
+                    remote(piece, slot.at[k], ss.at[t, k], rs.at[t, k], peers[k])
+                    for k, piece in enumerate(pieces)
+                ]
+
+            def into(dst, slot, count):
+                return functools.partial(add_into, dst, [slot.at[k] for k in range(count)])
+
+            def part(px, pz, py, p=p, g=g, i=i, core=c):
+                return view(lay, p, g, i, core, px, pz, py)
+
+            if 0 in stages:
+                slot = ca[g].at[i]
+                self.copies[t, 0] = [remote(part(ALL, ALL, ALL, core=1 - c), slot, c_s.at[t], c_r.at[t], cs[0])]
+                self.adds[t, 1] = functools.partial(add_into, part(ALL, ALL, ALL), [slot])
+            if 1 in stages and i < 2:
+                slot = ra1[g].at[i]
+                self.copies[t, 1] = along([part(k, ALL, ALL) for k in other_x], slot, xs, x_s, x_r)
+                self.adds[t, 2] = into(part(x, ALL, ALL), slot, lay.nx - 1)
+            elif 1 in stages:
+                slot = rb1[g].at[0]
+                self.copies[t, 1] = along([part(ALL, ALL, k) for k in other_y], slot, ys, y_s, y_r)
+                self.adds[t, 2] = into(part(ALL, ALL, y), slot, lay.ny - 1)
+            if 2 in stages and i < 2:
+                slot = ra2[g].at[i]
+                self.copies[t, 2] = along([part(x, ALL, k) for k in other_y], slot, ys, y_s, y_r)
+                self.adds[t, 3] = into(part(x, ALL, y), slot, lay.ny - 1)
+            elif 2 in stages:
+                slot = rb2[g].at[0]
+                self.copies[t, 2] = along([part(k, ALL, y) for k in other_x], slot, xs, x_s, x_r)
+                self.adds[t, 3] = into(part(x, ALL, y), slot, lay.nx - 1)
+            if 3 in stages:
+                slot = ra3[g].at[i]
+                self.copies[t, 3] = along([part(x, k, y) for k in other_z], slot, zs, z_s, z_r)
+                out = shard_view(lay, fs[g], g, i, c, x)
+                self.adds[t, 4] = functools.partial(
+                    set_sum, out, [part(x, z, y)] + [slot.at[k] for k in range(lay.nz - 1)]
+                )
+                self.copies[t, 4] = [
+                    remote(out, out, fx_s.at[t, k], fx_r.at[t, k], peer) for k, peer in enumerate(xs)
+                ]
+                both = shard_view(lay, fs[g], g, i, c, ALL)
+                self.copies[t, 5] = [remote(both, both, fc_s.at[t], fc_r.at[t], cs[0])]
+
+    def settle(self, t, k):
+        if k > 0:
+            arrive(self.copies[t, k - 1])
+            if (t, k) in self.adds:
+                self.adds[t, k]()
+
+    def begin(self, t, k):
+        start(self.copies[t, k])
+
+    def step(self, t, k):
+        self.settle(t, k)
+        if k < 6:
+            self.begin(t, k)
+
+    def drain(self):
+        for group in self.copies.values():
+            sent(group)
+
+
+def set_sum(out, srcs):
+    total = srcs[0][...].astype(F32)
+    for src in srcs[1:]:
+        total = total + src[...].astype(F32)
+    out[...] = total.astype(BF)
+
+
+def add_into(dst, srcs):
+    lead = dst.shape[:-2]
+
+    def body(j, carry):
+        index = []
+        rest = j
+        for size in reversed(lead):
+            index.append(lax.rem(rest, size))
+            rest = rest // size
+        index = tuple(reversed(index))
+        total = dst[index].astype(F32)
+        for src in srcs:
+            total = total + src[index].astype(F32)
+        dst[index] = total.astype(BF)
+        return carry
+
+    lax.fori_loop(0, math.prod(lead), body, 0)
+
+
 def rope(u, cos, low, high):
     return u * cos + pltpu.roll(u, LANES - 8, 1) * low + pltpu.roll(u, 8, 1) * high
 
@@ -211,9 +316,10 @@
     lay, rows,
     u_up, u_down, qkv, dense, tok, grad, seg, v0, v1, v2, v3, v4, v5, v6,
     g_up, g_down, p_out, prev_out, own_out, attn_hbm, vectors, up_add, att_sums,
-    small, u_att, p_att, fg_prev, fg_own, attn_out, g_att, g_small, tok_halo, seg_halo, first_all, first_t, q_s, k_s, v_s, do_s, ctx_s, ctx_t,
+    small, u_att, p_att, fg_prev, fg_own, attn_out, g_att, g_small, tok_halo, seg_halo, first_all, q_s, k_s, v_s, do_s, ctx_s, ctx_t,
     dq_s, dk_s, dv_s, cos_s, low_s, high_s, bias, dk_acc, dv_acc, qkv_add, s_s, w_s, d_s,
     local_sem, z_s, z_r, y_s, y_r, x_s, x_r, c_s, c_r, sm_s, sm_r, h_s, h_r, out_sem,
+    ca, ra1, rb1, rc_s, rc_r, rx_s, rx_r, ry_s, ry_r,
 ):
     span = 3 * rows
     r = qkv.shape[0]
@@ -365,7 +471,6 @@
     own_rows = pl.ds(2 * rows, rows)
     first = (norm_rows(tok[...]) * gain + shift).astype(BF)
     first_all[own_rows, :] = first
-    first_t[:, own_rows] = first.T
     pass_halo(0)
     arrive(segs)
     least = jnp.maximum(0, 2 * rows - b * rows)
@@ -430,13 +535,17 @@
     lax.fori_loop(0, 2, own_values, 0)
     own[0].wait_recv()
     net.pass_on(3, 1)
+
+    def earlier_norms(k):
+        for n in range(2):
+            near = pl.ds(k * half, half)
+            before = norm_rows(tok_halo[n, near, :]) * gain + shift
+            first_all[pl.ds(n * rows + k * half, half), :] = before.astype(BF)
+
+    earlier_norms(0)
     net.issue(8, 0)
     own[1].wait_recv()
-    for k in range(2):
-        at = slice(k * rows, (k + 1) * rows)
-        before = (norm_rows(tok_halo[k]) * gain + shift).astype(BF)
-        first_all[at, :] = before
-        first_t[:, at] = before.T
+    earlier_norms(1)
     net.pass_on(4, 1)
     net.pass_on(5, 2)
 
@@ -538,6 +647,48 @@
 
     lax.fori_loop(0, PAIRS, pair, 0)
 
+    sums = Reduce(
+        lay, (p_att,), None, ((ca,), (ra1,), (rb1,), None, None, None),
+        (rc_s, rc_r, rx_s, rx_r, ry_s, ry_r) + (None,) * 6, {0: (0, 1), 1: (0,), 2: (0, 1)},
+    )
+    outs = []
+
+    def leave(i):
+        cols = pl.ds(1024 * i, 1024)
+        copy = pltpu.make_async_copy(p_att.at[:, :, :, cols], p_out.at[:, :, :, cols], out_sem.at[i])
+        copy.start()
+        outs.append(copy)
+
+    def put(kind, j, value):
+        p_att[:, :, :, kind * D + 256 * j : kind * D + 256 * (j + 1)] = value.astype(BF).reshape(
+            lay.nz, lay.ny, r, 256
+        )
+
+    def tile_of(ref, j):
+        return ref[:, slice(256 * j, 256 * (j + 1))]
+
+    def weight_grad(kind, j):
+        if kind == 0:
+            put(0, j, mm(first_all[own_rows, :], tile_of(dq_s, j), TN))
+        elif kind == 3:
+            put(3, j, mm(ctx_t[...], tile_of(grad, j)))
+        else:
+            put(kind, j, mm(first_all[...], tile_of((dk_s, dv_s)[kind - 1], j), TN))
+
+    for kind, j in ((1, 0), (0, 0), (0, 1), (0, 2)):
+        weight_grad(kind, j)
+    sums.step(0, 0)
+    for kind, j in ((2, 2), (3, 0), (3, 1), (3, 2)):
+        weight_grad(kind, j)
+    sums.step(0, 1)
+    sums.step(2, 0)
+    for kind, j in ((1, 1), (1, 2)):
+        weight_grad(kind, j)
+    sums.step(2, 1)
+    for kind, j in ((2, 0), (2, 1)):
+        weight_grad(kind, j)
+    sums.step(1, 0)
+
     def earlier_grad(k, carry):
         at = pl.ds(pl.multiple_of(k * 256, 256), 256)
         value = mm(dk_s[at, :], weight(D, D), NT) + mm(dv_s[at, :], weight(2 * D, D), NT)
@@ -545,8 +696,10 @@
         return carry
 
     lax.fori_loop(0, 2 * rows // 256, earlier_grad, 0)
-    outs = [pltpu.make_async_copy(fg_prev, prev_out, out_sem.at[0])]
-    outs[0].start()
+    outs.append(pltpu.make_async_copy(fg_prev, prev_out, out_sem.at[3]))
+    outs[-1].start()
+    sums.settle(1, 1)
+    leave(1)
     for k in range(rows // 256):
         at = slice(2 * rows + 256 * k, 2 * rows + 256 * (k + 1))
         near = slice(256 * k, 256 * (k + 1))
@@ -555,33 +708,25 @@
             + mm(dv_s[at, :], weight(2 * D, D), NT)
             + mm(dq_s[near, :], weight(0, D), NT)
         )
-
-    outs.append(pltpu.make_async_copy(fg_own, own_out, out_sem.at[1]))
-    outs[1].start()
-
-    def weight_grads(j, carry):
+    outs.append(pltpu.make_async_copy(fg_own, own_out, out_sem.at[4]))
+    outs[-1].start()
+
+    def attention_out(j, carry):
         col = pl.multiple_of(256 * j, 256)
-        cols = pl.ds(col, 256)
-
-        def put(kind, value):
-            p_att[:, :, :, pl.ds(pl.multiple_of(kind * D + col, 256), 256)] = value.astype(BF).reshape(
-                lay.nz, lay.ny, r, 256
-            )
-
-        put(0, mm(first_t[:, own_rows], dq_s[:, cols]))
-        put(1, mm(first_t[...], dk_s[:, cols]))
-        put(2, mm(first_t[...], dv_s[:, cols]))
-        put(3, mm(ctx_t[...], grad[:, cols]))
-        attn_out[:, cols] = mm(ctx_s[...], weight(pl.multiple_of(3 * D + col, 256), 256))
+        attn_out[:, pl.ds(col, 256)] = mm(ctx_s[...], weight(pl.multiple_of(3 * D + col, 256), 256))
         return carry
 
-    lax.fori_loop(0, 3, weight_grads, 0)
-    outs.append(pltpu.make_async_copy(p_att, p_out, out_sem.at[2]))
-    outs.append(pltpu.make_async_copy(attn_out, attn_hbm, out_sem.at[3]))
-    start(outs[2:])
+    lax.fori_loop(0, 3, attention_out, 0)
+    outs.append(pltpu.make_async_copy(attn_out, attn_hbm, out_sem.at[5]))
+    outs[-1].start()
     for k, ref in enumerate((dq_s, dk_s, dv_s)):
         att_sums[k : k + 1, :] = jnp.sum(ref[...].astype(F32), 0, keepdims=True)
     att_sums[3:8, :] = jnp.zeros((5, D), F32)
+    sums.settle(0, 2)
+    leave(0)
+    sums.settle(2, 2)
+    leave(2)
+    sums.drain()
     for t in range(3, 9):
         net.done(t)
     net.drain()
@@ -621,126 +766,22 @@
         scratch_shapes=[
             v((SMALL_ROWS, LANES), F32), v((r, 4 * D)), v(grad_shape(lay, 0, r)), v((2 * rows, D)), v((rows, D), F32), v((rows, D), F32),
             v(grad_shape(lay, 0, r)), v((lay.nz, lay.ny, SMALL_ROWS, LANES), F32), v((2, rows, D)),
-            v((2, 1, rows), jnp.int32), v((span, D)), v((D, span)), v((rows, D)), v((span, D)),
+            v((2, 1, rows), jnp.int32), v((span, D)), v((rows, D)), v((span, D)),
             v((span, D)), v((rows, D)), v((rows, D)), v((D, rows)), v((rows, D)), v((span, D)),
             v((span, D)), v((span, LANES), F32), v((span, LANES), F32), v((span, LANES), F32),
             v((span, rows), F32), v((span, LANES), F32), v((span, LANES), F32), v((1, 3 * D), F32),
             v((2, span, 256), F32), v((2, span, 256)), v((2, span, 256)),
             dma(n + 1), dma(n, lz), dma(n, lz), dma(n, ly), dma(n, ly), dma(n, lx), dma(n, lx),
-            dma(n), dma(n), dma(lay.nz + ly), dma(lay.nz + ly), dma(6), dma(6), dma(4),
+            dma(n), dma(n), dma(lay.nz + ly), dma(lay.nz + ly), dma(6), dma(6), dma(6),
+            v((3,) + part_shape(lay, 0, True, True, True, r)),
+            v((1, lx) + part_shape(lay, 0, False, True, True, r)),
+            v((1, ly) + part_shape(lay, 0, True, True, False, r)),
+            dma(3), dma(3), dma(3, lx), dma(3, lx), dma(3, ly), dma(3, ly),
         ],
         compiler_params=pltpu.CompilerParams(
             collective_id=0, has_side_effects=True, vmem_limit_bytes=VMEM_LIMIT
         ),
     )(u_up, u_down, qkv, dense, tok, grad, seg, *vectors)
-
-
-class Reduce:
-    def __init__(self, lay, ps, fs, bufs, sems):
-        (ca, ra1, rb1, ra2, rb2, ra3) = bufs
-        (c_s, c_r, x_s, x_r, y_s, y_r, z_s, z_r, fx_s, fx_r, fc_s, fc_r) = sems
-        x, c, z, y = lay.coords()
-        xs, cs, zs, ys = line_peers(lay)
-        self.steps = []
-        for t, (g, i) in enumerate(CHUNKS):
-            p, f = ps[g], fs[g]
-            other_x = [wrap(x + 1 + k, lay.nx) for k in range(lay.nx - 1)]
-            other_y = [wrap(y + 1 + k, lay.ny) for k in range(lay.ny - 1)]
-            other_z = [wrap(z + 1 + k, lay.nz) for k in range(lay.nz - 1)]
-
-            def over_x(pieces, slot):
-                return [
-                    remote(piece, slot.at[k], x_s.at[t, k], x_r.at[t, k], xs[k])
-                    for k, piece in enumerate(pieces)
-                ]
-
-            def over_y(pieces, slot):
-                return [
-                    remote(piece, slot.at[k], y_s.at[t, k], y_r.at[t, k], ys[k])
-                    for k, piece in enumerate(pieces)
-                ]
-
-            def into(dst, slot, count):
-                return functools.partial(add_into, dst, [slot.at[k] for k in range(count)])
-
-            core_slot = ca[g].at[i]
-            core = [
-                remote(view(lay, p, g, i, 1 - c, ALL, ALL, ALL), core_slot, c_s.at[t], c_r.at[t], cs[0])
-            ]
-            add_core = functools.partial(add_into, view(lay, p, g, i, c, ALL, ALL, ALL), [core_slot])
-            if i < 2:
-                slot1, slot2 = ra1[g].at[i], ra2[g].at[i]
-                first = over_x([view(lay, p, g, i, c, k, ALL, ALL) for k in other_x], slot1)
-                add_1 = into(view(lay, p, g, i, c, x, ALL, ALL), slot1, lay.nx - 1)
-                second = over_y([view(lay, p, g, i, c, x, ALL, k) for k in other_y], slot2)
-                add_2 = into(view(lay, p, g, i, c, x, ALL, y), slot2, lay.ny - 1)
-            else:
-                slot1, slot2 = rb1[g].at[0], rb2[g].at[0]
-                first = over_y([view(lay, p, g, i, c, ALL, ALL, k) for k in other_y], slot1)
-                add_1 = into(view(lay, p, g, i, c, ALL, ALL, y), slot1, lay.ny - 1)
-                second = over_x([view(lay, p, g, i, c, k, ALL, y) for k in other_x], slot2)
-                add_2 = into(view(lay, p, g, i, c, x, ALL, y), slot2, lay.nx - 1)
-            slot3 = ra3[g].at[i]
-            third = [
-                remote(view(lay, p, g, i, c, x, k, y), slot3.at[n], z_s.at[t, n], z_r.at[t, n], zs[n])
-                for n, k in enumerate(other_z)
-            ]
-            out = shard_view(lay, f, g, i, c, x)
-            own = view(lay, p, g, i, c, x, z, y)
-            finish = functools.partial(
-                set_sum, out, [own] + [slot3.at[k] for k in range(lay.nz - 1)]
-            )
-            share_x = [
-                remote(out, out, fx_s.at[t, k], fx_r.at[t, k], peer) for k, peer in enumerate(xs)
-            ]
-            both = shard_view(lay, f, g, i, c, ALL)
-            share_c = [remote(both, both, fc_s.at[t], fc_r.at[t], cs[0])]
-            self.steps.append(
-                (
-                    (core, first, second, third, share_x, share_c),
-                    (None, add_core, add_1, add_2, finish, None),
-                )
-            )
-
-    def step(self, t, k):
-        copies, adds = self.steps[t]
-        if k > 0:
-            arrive(copies[k - 1])
-        if k < len(copies):
-            if adds[k] is not None:
-                adds[k]()
-            start(copies[k])
-
-    def drain(self):
-        for copies, _ in self.steps:
-            for group in copies:
-                sent(group)
-
-
-def set_sum(out, srcs):
-    total = srcs[0][...].astype(F32)
-    for src in srcs[1:]:
-        total = total + src[...].astype(F32)
-    out[...] = total.astype(BF)
-
-
-def add_into(dst, srcs):
-    lead = dst.shape[:-2]
-
-    def body(j, carry):
-        index = []
-        rest = j
-        for size in reversed(lead):
-            index.append(lax.rem(rest, size))
-            rest = rest // size
-        index = tuple(reversed(index))
-        total = dst[index].astype(F32)
-        for src in srcs:
-            total = total + src[index].astype(F32)
-        dst[index] = total.astype(BF)
-        return carry
-
-    lax.fori_loop(0, math.prod(lead), body, 0)
 
 
 def norm_back(grad, gain, normed, factor):
@@ -803,15 +844,15 @@
     start(taken[4:])
     start(loads[1])
     barrier_with(xs + cs + zs + ys + around)
+    wanted = {t: (0, 1, 2, 3) for t in range(3, len(CHUNKS))}
+    wanted.update({0: (2, 3), 1: (1, 2, 3), 2: (2, 3)})
     net = Reduce(
-        lay, (p_att, p_up, p_down), (f_att, f_up, f_down), (ca, ra1, rb1, ra2, rb2, ra3), sems[:12]
+        lay, (p_att, p_up, p_down), (f_att, f_up, f_down),
+        ((None,) + tuple(ca), ra1, (None,) + tuple(rb1), ra2, rb2, ra3), sems[:12], wanted,
     )
-    for t in range(3):
+    for t, k in ((1, 1), (2, 2), (0, 2)):
         taken[t].wait()
-        net.step(t, 0)
-    net.step(0, 1)
-    net.step(1, 1)
-    net.step(2, 1)
+        net.begin(t, k)
     taken[3].wait()
     even = lax.rem(b, 2) == 0
     quarter = rows // 4
@@ -844,6 +885,7 @@
         to_owner[k].start()
 
     hop_halo(0)
+    hop_halo(1)
 
     gain_first, gain_second = vectors[0:1, :], vectors[2:3, :]
     normed, factor = norm_parts(tok[...].astype(F32))
@@ -861,14 +903,14 @@
 
     step = net.step
     events = [
-        [(hop_halo, 1)],
         [],
-        [(step, 2, 2)],
-        [(step, 3, 0), (step, 0, 2)],
-        [(step, 3, 1), (forward_halo, 0), (hop_halo, 2)],
-        [(step, 4, 0), (step, 1, 2)],
-        [(step, 4, 1), (forward_halo, 1), (hop_halo, 3), (step, 2, 3)],
-        [(step, 5, 0), (step, 6, 0), (step, 7, 0), (step, 8, 0), (step, 0, 3)],
+        [(step, 0, 3)],
+        [(hop_halo, 2)],
+        [(step, 3, 0), (step, 1, 2), (forward_halo, 0)],
+        [(step, 3, 1), (step, 2, 3), (hop_halo, 3)],
+        [(step, 4, 0), (forward_halo, 1)],
+        [(step, 4, 1), (step, 0, 4)],
+        [(step, 5, 0), (step, 6, 0), (step, 7, 0), (step, 8, 0), (step, 2, 4)],
     ]
     root = math.sqrt(0.5)
     level = 1.0 / math.sqrt(2.0 * math.pi)
@@ -922,13 +964,12 @@
 
     squares = lax.fori_loop(0, FF_CHUNKS, chunk, jnp.zeros((rows, 1), F32))
     run = lambda *pairs: [step(t, k) for t, k in pairs]
-    run((5, 1), (6, 1), (3, 2))
+    run((5, 1), (6, 1), (3, 2), (1, 3))
     output[...] = output_base[...].astype(BF)
     forward_halo(2)
-    run((1, 3), (8, 1), (7, 1), (2, 4))
     cot_sum = jnp.sum(grad[...].astype(F32), 0, keepdims=True)
-    run((0, 4))
     forward_halo(3)
+    run((4, 2), (5, 2), (7, 1), (8, 1), (1, 4))
 
     def put(k, value):
         v_c[c, k : k + 1, :] = value
@@ -943,7 +984,6 @@
     member = jnp.where((docs_of == doc) & (doc < docs), 1.0, 0.0)
     put(12, jnp.sum(token_norm * member, 0, keepdims=True))
     put(13, jnp.sum(member, 0, keepdims=True))
-    run((4, 2))
     keep = jnp.where(even, 1.0, 0.0).astype(F32)
 
     def norms(k):
@@ -964,14 +1004,14 @@
         return [p + q for p, q in zip(left, right)]
 
     sums = norms(0)
-    run((5, 2), (1, 4))
+    run((3, 3))
     sums = add_up(sums, norms(1))
-    run((6, 2), (3, 3))
+    run((6, 2))
     sums = add_up(sums, norms(2))
     sums = add_up(sums, norms(3))
     for k in range(4):
         put(k, sums[k])
-    run((8, 2))
+    run((4, 3))
 
     at = [0, 1, lay.nx, lay.nx + lay.ny - 1]
 
@@ -993,22 +1033,22 @@
         return value
 
     start(vec_c)
-    run((7, 2), (4, 3))
+    run((5, 3), (7, 2))
     arrive(vec_c)
     v_x[x] = add_all(v_c, 2)
     start(vec_x)
-    run((2, 5), (0, 5), (3, 4), (6, 3), (5, 3))
+    run((3, 4), (8, 2), (6, 3))
     arrive(vec_x)
     v_y[y] = add_all(v_x, lay.nx)
     start(vec_y)
-    run((1, 5), (8, 3), (4, 4), (3, 5), (7, 3))
+    run((4, 4), (7, 3), (8, 3), (5, 4))
     arrive(vec_y)
     v_z[z] = add_all(v_y, lay.ny)
     start(vec_z)
-    run((6, 4), (5, 4), (4, 5), (8, 4), (6, 5), (5, 5), (7, 4), (8, 5))
+    run((6, 4), (0, 5), (1, 5), (2, 5), (3, 5), (4, 5), (5, 5), (7, 4), (6, 5), (8, 4))
     arrive(vec_z)
     vec_out[...] = add_all(v_z, lay.nz)
-    run((7, 5))
+    run((7, 5), (8, 5))
     for t in range(9):
         net.step(t, 6)
     net.drain()
@@ -1034,8 +1074,10 @@
     def v(shape, dtype=BF):
         return pltpu.VMEM(shape, dtype)
 
-    def bufs(chunks, peers, x_all, z_all, y_all):
-        return [v((chunks,) + peers + part_shape(lay, g, x_all, z_all, y_all, r)) for g in range(3)]
+    def bufs(chunks, peers, x_all, z_all, y_all, first=0):
+        return [
+            v((chunks,) + peers + part_shape(lay, g, x_all, z_all, y_all, r)) for g in range(first, 3)
+        ]
 
     scratch = [
         v(grad_shape(lay, 0, r)), v((2 * rows, D)), v((rows, D), F32), v((rows, D), F32),
@@ -1043,9 +1085,9 @@
         v((2, lay.nz, lay.ny, r, D)), v((2, lay.nz // FF_CHUNKS, lay.ny, 4, r, D)),
         v((rows, D)), v((D, rows)), v((rows, D)), v((rows, D)), v((rows, D), F32),
         v((rows, D)), v((rows, D)),
-        bufs(3, (), True, True, True),
+        bufs(3, (), True, True, True, 1),
         bufs(2, (lx,), False, True, True),
-        bufs(1, (ly,), True, True, False),
+        bufs(1, (ly,), True, True, False, 1),
         bufs(2, (ly,), False, True, False),
         bufs(1, (lx,), False, True, False),
         bufs(3, (lz,), False, False, False),

time: 232 us -> 224 us (0.966)
  Pallas kernels: 231 us -> 223 us
    pallas_call x1, Pallas kernels: 101 us -> 89.5 us  [back(): pl.pallas_call(functools.partial(back_kernel, lay, rows, docs), name='bac...]
    pallas_call x1, Pallas kernels: 125 us -> 129 us  [front(): pl.pallas_call(functools.partial(front_kernel, lay, rows), name='front',...]
where the time goes in v4:
time: 224 us
  Pallas kernels  223 us (100%)
    pallas_call x1, Pallas kernels, front(): pl.pallas_call(functools.partial(front_kernel, lay, rows), name='front',...  129 us
    pallas_call x1, Pallas kernels, back(): pl.pallas_call(functools.partial(back_kernel, lay, rows, docs), name='bac...  89.5 us

profile of v4, /device:TPU:1, one launch (start us, length us, event | category | flops | bytes accessed | tf_op | source)
XLA Modules:
  0.0 224.1 jit_solution(11347027028565397883)
XLA Ops:
  0.6 129.2 %front.1 = (bf16[4,2,96,3072]{3,2,1,0:T(8,128)(2,1)}, bf16[4,2,4,96,768]{4,3,2,1,0:T(8,128)(2,1)}, bf16[4,2,96,3072]{3,2,1,0:T(8,128)(2,1)}, bf16[1024,768]{1,0:...) custom-call(bf16[96,3072]{1,0:T(8,128)(2,1)} %u_up.1, ...), custom_call_target="tpu_custom_call" | custom-call | tf_op jit(solution)/shard_map/front/pallas_call | solution.py:760
  129.9 89.5 %back.1 = (bf16[512,768]{1,0:T(8,128)(2,1)}, bf16[512,768]{1,0:T(8,128)(2,1)}, bf16[96,3072]{1,0:T(8,128)(2,1)}, bf16[96,3072]{1,0:T(8,128)(2,1)}, bf16[4,96,768]{2,1,0:T(8,128)(2,1)}, /*index=5*/f32[16,768]{1,0:T(8,128)}) custom-call(bf16[4,2,96,3072]{3,2,1,0:T(8,128)(2,1)} %get-tuple-element.43.g_up, bf16[4,2,4,96,768]{4,3,2,1,0:T(8,128)(2,1)} %get-tuple-element.44.g_down, ...), custom_call_target="tpu_custom_call" | custom-call | tf_op jit(solution)/shard_map/back/pallas_call | solution.py:1102
  219.4 4.5 %finish.1 = (bf16[512,768]{1,0:T(8,128)(2,1)}, bf16[512,768]{1,0:T(8,128)(2,1)}, f32[96]{0:T(128)}, f32[96]{0:T(128)}, f32[96]{0:T(128)}, /*index=5*/f32[96]{0:T...) custom-call(bf16[96,3072]{1,0:T(8,128)(2,1)} %get-tuple-element.52.f, ...), custom_call_target="tpu_custom_call" | custom-call | tf_op jit(solution)/shard_map/finish/pallas_call | solution.py:1162

commit v5 on v4

--- a/solution.py
+++ b/solution.py
@@ -563,17 +563,11 @@
     go, send, end = net.pass_on, net.issue, net.done
     later = [
         [(go, 8, 1), (send, 7, 0), (go, 4, 2)],
-        [(go, 5, 3)],
-        [(go, 6, 1)],
-        [(go, 3, 3), (go, 7, 1)],
+        [(go, 5, 3), (go, 6, 1), (go, 3, 3), (go, 7, 1)],
         [(go, 8, 2), (go, 6, 2)],
         [(go, 4, 3), (go, 7, 2)],
-        [],
-        [(go, 8, 3)],
-        [],
-        [(go, 6, 3)],
+        [(go, 8, 3), (go, 6, 3)],
         [(go, 7, 3)],
-        [],
     ]
     tile = 256
 
@@ -583,66 +577,97 @@
         do_t = do_s[:, lanes].astype(F32).T
         lane = lax.broadcasted_iota(jnp.int32, (tile, LANES), 1)
         zero = jnp.zeros((), BF)
-        for t in range(rows // tile):
+        units = [(t, hh) for t in range(rows // tile) for hh in range(2)]
+        count = len(units)
+        tops, totals, norms = [None] * count, [None] * count, [None] * count
+        outs, dqs = [None] * count, [None] * count
+        written = set()
+
+        def masked(ref, u):
+            t, hh = units[u]
+            return jnp.where((lane // HD) == hh, ref[t * tile : (t + 1) * tile, lanes], zero)
+
+        def pieces(u):
+            kl = 2 * rows + (units[u][0] + 1) * tile
+            return [slice(k * LANES, (k + 1) * LANES) for k in range(kl // LANES)]
+
+        def scores(u, at, qm):
+            t = units[u][0]
+            st = mm(k_s[at, lanes], qm, NT) + bias[at, t * tile : (t + 1) * tile]
+            s_s[u % 2, at, :] = st
+            most = jnp.max(st, 0, keepdims=True)
+            tops[u] = most if tops[u] is None else jnp.maximum(tops[u], most)
+
+        def exponents(u, at):
+            e = jnp.exp(s_s[u % 2, at, :] - tops[u])
+            s_s[u % 2, at, :] = e
+            part = jnp.sum(e, 0, keepdims=True)
+            totals[u] = part if totals[u] is None else totals[u] + part
+
+        def key_value_grads(u, at, qm, dom):
+            dk, dv = mm(d_s[u % 2, at, :], qm), mm(w_s[u % 2, at, :], dom)
+            if at.start in written:
+                dk_acc[at, :] += dk
+                dv_acc[at, :] += dv
+            else:
+                dk_acc[at, :] = dk
+                dv_acc[at, :] = dv
+                written.add(at.start)
+
+        qm = masked(q_s, 0)
+        for at in pieces(0):
+            scores(0, at, qm)
+        for u in range(count):
+            t, hh = units[u]
+            part = slice(hh * HD, (hh + 1) * HD)
             cols = slice(t * tile, (t + 1) * tile)
             kl = 2 * rows + (t + 1) * tile
-            pieces = [slice(k * tile, (k + 1) * tile) for k in range(kl // tile)]
-            qms = [jnp.where((lane // HD) == hh, q_s[cols, lanes], zero) for hh in range(2)]
-            doms = [jnp.where((lane // HD) == hh, do_s[cols, lanes], zero) for hh in range(2)]
-            tops, norms = [], []
-            for hh in range(2):
-                top = None
-                for at in pieces:
-                    st = mm(k_s[at, lanes], qms[hh], NT) + bias[at, cols]
-                    s_s[hh, at, :] = st
-                    most = jnp.max(st, 0, keepdims=True)
-                    top = most if top is None else jnp.maximum(top, most)
-                tops.append(top)
-            for hh in range(2):
-                total_e = None
-                for at in pieces:
-                    e = jnp.exp(s_s[hh, at, :] - tops[hh])
-                    s_s[hh, at, :] = e
-                    part = jnp.sum(e, 0, keepdims=True)
-                    total_e = part if total_e is None else total_e + part
-                norms.append(1.0 / total_e)
-            outs, dqs = [], []
-            for hh in range(2):
-                for at in pieces:
-                    w_s[hh, at, :] = (s_s[hh, at, :] * norms[hh]).astype(BF)
-            for hh in range(2):
-                part = slice(hh * HD, (hh + 1) * HD)
-                o_t = mm(v_t[part, :kl], w_s[hh, :kl, :])
-                delta = jnp.sum(o_t * do_t[part, cols], 0, keepdims=True)
-                outs.append(o_t)
-                for at in pieces:
-                    dp = mm(v_s[at, lanes], doms[hh], NT)
-                    d_s[hh, at, :] = ((s_s[hh, at, :] * norms[hh]) * (dp - delta)).astype(BF)
-                dqs.append(mm(k_t[part, :kl], d_s[hh, :kl, :]))
-            for k, at in enumerate(pieces):
-                dk = mm(d_s[0, at, :], qms[0]) + mm(d_s[1, at, :], qms[1])
-                dv = mm(w_s[0, at, :], doms[0]) + mm(w_s[1, at, :], doms[1])
-                if t == 0 or k == len(pieces) - 1:
-                    dk_acc[at, :] = dk
-                    dv_acc[at, :] = dv
-                else:
-                    dk_acc[at, :] += dk
-                    dv_acc[at, :] += dv
-            o_pair = jnp.concatenate(outs, 0)
+            mine = pieces(u)
+            after = pieces(u + 1) if u + 1 < count else []
+            before = pieces(u - 1) if u > 0 else []
+            if after:
+                qm = masked(q_s, u + 1)
+            for k in range(max(len(mine), len(after))):
+                if k < len(after):
+                    scores(u + 1, after[k], qm)
+                if k < len(mine):
+                    exponents(u, mine[k])
+            norms[u] = 1.0 / totals[u]
+            if before:
+                q_last, do_last = masked(q_s, u - 1), masked(do_s, u - 1)
+            for k in range(max(len(mine), len(before))):
+                if k < len(before):
+                    key_value_grads(u - 1, before[k], q_last, do_last)
+                if k < len(mine):
+                    w_s[u % 2, mine[k], :] = (s_s[u % 2, mine[k], :] * norms[u]).astype(BF)
+            o_t = mm(v_t[part, :kl], w_s[u % 2, :kl, :])
+            delta = jnp.sum(o_t * do_t[part, cols], 0, keepdims=True)
+            outs[u] = o_t
+            dom = masked(do_s, u)
+            for at in mine:
+                dp = mm(v_s[at, lanes], dom, NT)
+                d_s[u % 2, at, :] = ((s_s[u % 2, at, :] * norms[u]) * (dp - delta)).astype(BF)
+            dqs[u] = mm(k_t[part, :kl], d_s[u % 2, :kl, :])
+            if hh == 0:
+                continue
+            o_pair = jnp.concatenate(outs[u - 1 : u + 1], 0)
             ctx_t[lanes, cols] = o_pair.astype(BF)
             ctx_s[cols, lanes] = o_pair.T.astype(BF)
-            dq = jnp.concatenate(dqs, 0).T * scale
+            dq = jnp.concatenate(dqs[u - 1 : u + 1], 0).T * scale
             at = slice(2 * rows + t * tile, 2 * rows + (t + 1) * tile)
             dq_s[cols, lanes] = rope(dq, cos_s[at, :], -low_s[at, :], -high_s[at, :]).astype(BF)
-            for k in range(PAIRS):
-
-                @pl.when(p == k)
-                def _(k=k, t=t):
-                    for event, *where in later[2 * k + t]:
-                        event(*where)
-
+        q_last, do_last = masked(q_s, count - 1), masked(do_s, count - 1)
+        for at in pieces(count - 1):
+            key_value_grads(count - 1, at, q_last, do_last)
         dk_s[:, lanes] = rope(dk_acc[...], cos_s[...], -low_s[...], -high_s[...]).astype(BF)
         dv_s[:, lanes] = dv_acc[...].astype(BF)
+        for k in range(PAIRS):
+
+            @pl.when(p == k)
+            def _(k=k):
+                for event, *where in later[k]:
+                    event(*where)
+
         return carry
 
     lax.fori_loop(0, PAIRS, pair, 0)
@@ -799,11 +824,11 @@
 def back_kernel(
     lay, rows, docs,
     g_up, g_down, p_in, prev_in, own_in, attn_in, vectors, up_add, att_sums, tok, grad, seg,
-    output, input_grad, f_att, f_up, f_down, vec_out,
-    p_att, fg_prev, fg_own, attn_out, p_up, p_down, w_up, w_down, second_in, second_t, act_s, pg_s, sg_acc, hop, home,
+    out_hbm, input_hbm, att_hbm, up_hbm, down_hbm, vec_out,
+    output, input_grad, f_att, f_up, f_down, p_att, fg_prev, fg_own, attn_out, p_up, p_down, w_up, w_down, second_in, second_t, act_s, pg_s, sg_acc, hop, home,
     ca, ra1, rb1, ra2, rb2, ra3, v_c, v_x, v_y, v_z, *sems,
 ):
-    (c_s, c_r, x_s, x_r, y_s, y_r, z_s, z_r, fx_s, fx_r, fc_s, fc_r, v_s, v_r, w_sem, h_s, h_r, in_sem) = sems
+    (c_s, c_r, x_s, x_r, y_s, y_r, z_s, z_r, fx_s, fx_r, fc_s, fc_r, v_s, v_r, w_sem, h_s, h_r, in_sem, out_sem) = sems
     r = p_in.shape[2]
     x, c, z, y = lay.coords()
     xs, cs, zs, ys = line_peers(lay)
@@ -966,11 +991,17 @@
     run = lambda *pairs: [step(t, k) for t, k in pairs]
     run((5, 1), (6, 1), (3, 2), (1, 3))
     output[...] = output_base[...].astype(BF)
+    left = []
+
+    def leave(k, ref, target):
+        copy = pltpu.make_async_copy(ref, target, out_sem.at[k])
+        copy.start()
+        left.append(copy)
+
+    leave(0, output, out_hbm)
     forward_halo(2)
     cot_sum = jnp.sum(grad[...].astype(F32), 0, keepdims=True)
     forward_halo(3)
-    run((4, 2), (5, 2), (7, 1), (8, 1), (1, 4))
-
     def put(k, value):
         v_c[c, k : k + 1, :] = value
 
@@ -984,6 +1015,7 @@
     member = jnp.where((docs_of == doc) & (doc < docs), 1.0, 0.0)
     put(12, jnp.sum(token_norm * member, 0, keepdims=True))
     put(13, jnp.sum(member, 0, keepdims=True))
+    run((4, 2), (5, 2), (7, 1), (8, 1), (1, 4))
     keep = jnp.where(even, 1.0, 0.0).astype(F32)
 
     def norms(k):
@@ -1009,6 +1041,7 @@
     run((6, 2))
     sums = add_up(sums, norms(2))
     sums = add_up(sums, norms(3))
+    leave(1, input_grad, input_hbm)
     for k in range(4):
         put(k, sums[k])
     run((4, 3))
@@ -1033,27 +1066,32 @@
         return value
 
     start(vec_c)
-    run((5, 3), (7, 2))
+    run((5, 3), (8, 2))
     arrive(vec_c)
     v_x[x] = add_all(v_c, 2)
     start(vec_x)
-    run((3, 4), (8, 2), (6, 3))
+    run((7, 2), (3, 4), (6, 3), (8, 3), (7, 3))
     arrive(vec_x)
     v_y[y] = add_all(v_x, lay.nx)
     start(vec_y)
-    run((4, 4), (7, 3), (8, 3), (5, 4))
+    run((4, 4), (5, 4))
     arrive(vec_y)
     v_z[z] = add_all(v_y, lay.ny)
     start(vec_z)
-    run((6, 4), (0, 5), (1, 5), (2, 5), (3, 5), (4, 5), (5, 5), (7, 4), (6, 5), (8, 4))
+    run((6, 4), (0, 5), (1, 5), (2, 5), (3, 5), (4, 5), (5, 5), (8, 4))
+    run((0, 6), (1, 6), (2, 6))
+    leave(2, f_att, att_hbm)
+    run((6, 5), (3, 6), (4, 6), (5, 6), (7, 4))
+    leave(3, f_up, up_hbm)
     arrive(vec_z)
     vec_out[...] = add_all(v_z, lay.nz)
-    run((7, 5), (8, 5))
-    for t in range(9):
-        net.step(t, 6)
+    run((8, 5), (7, 5), (6, 6), (8, 6), (7, 6))
+    leave(4, f_down, down_hbm)
     net.drain()
     sent(vec_c + vec_x + vec_y + vec_z)
     sent(to_next + to_owner)
+    for copy in left:
+        copy.wait()
 
 
 def back(lay, g_up, g_down, p_att, fg_prev, fg_own, attn_out, vectors, up_add, att_sums, tok, grad, seg):
@@ -1080,6 +1118,7 @@
         ]
 
     scratch = [
+        v((rows, D)), v((rows, D)), v((r, 4 * D)), v((r, 4 * D)), v((4, r, D)),
         v(grad_shape(lay, 0, r)), v((2 * rows, D)), v((rows, D), F32), v((rows, D), F32),
         v(grad_shape(lay, 1, r)), v(grad_shape(lay, 2, r)),
         v((2, lay.nz, lay.ny, r, D)), v((2, lay.nz // FF_CHUNKS, lay.ny, 4, r, D)),
@@ -1096,7 +1135,7 @@
     nv = 1 + lay.nx + lay.ny + lay.nz
     sems = [
         dma(n), dma(n), dma(n, lx), dma(n, lx), dma(n, ly), dma(n, ly), dma(n, lz), dma(n, lz),
-        dma(n, lx), dma(n, lx), dma(n), dma(n), dma(nv), dma(nv), dma(2, FF_CHUNKS), dma(8), dma(8), dma(6),
+        dma(n, lx), dma(n, lx), dma(n), dma(n), dma(nv), dma(nv), dma(2, FF_CHUNKS), dma(8), dma(8), dma(6), dma(5),
     ]
     vmem = pl.BlockSpec(memory_space=pltpu.VMEM)
     return pl.pallas_call(
@@ -1104,7 +1143,7 @@
         name="back",
         out_shape=outs,
         in_specs=hbm(6) + [vmem] * 6,
-        out_specs=(vmem,) * 6,
+        out_specs=tuple(hbm(5)) + (vmem,),
         scratch_shapes=scratch + vecs + sems,
         compiler_params=pltpu.CompilerParams(
             collective_id=1, has_side_effects=True, vmem_limit_bytes=VMEM_LIMIT

time: 224 us -> 213 us (0.951)
  Pallas kernels: 223 us -> 212 us
    pallas_call x1, Pallas kernels: 129 us -> 119 us  [front(): pl.pallas_call(functools.partial(front_kernel, lay, rows), name='front',...]
where the time goes in v5:
time: 213 us
  Pallas kernels  212 us (100%)
    pallas_call x1, Pallas kernels, front(): pl.pallas_call(functools.partial(front_kernel, lay, rows), name='front',...  119 us
    pallas_call x1, Pallas kernels, back(): pl.pallas_call(functools.partial(back_kernel, lay, rows, docs), name='bac...  89.2 us
    pallas_call x1, Pallas kernels, finish(): pl.pallas_call(functools.partial(finish_kernel, lay, docs, r), name='fini...  4.46 us

profile of v5, /device:TPU:1, one launch (start us, length us, event | category | flops | bytes accessed | tf_op | source)
XLA Modules:
  0.0 213.3 jit_solution(10832063599017978787)
XLA Ops:
  0.6 118.8 %front.1 = (bf16[4,2,96,3072]{3,2,1,0:T(8,128)(2,1)}, bf16[4,2,4,96,768]{4,3,2,1,0:T(8,128)(2,1)}, bf16[4,2,96,3072]{3,2,1,0:T(8,128)(2,1)}, bf16[1024,768]{1,0:...) custom-call(bf16[96,3072]{1,0:T(8,128)(2,1)} %u_up.1, ...), custom_call_target="tpu_custom_call" | custom-call | tf_op jit(solution)/shard_map/front/pallas_call | solution.py:785
  119.4 89.2 %back.1 = (bf16[512,768]{1,0:T(8,128)(2,1)}, bf16[512,768]{1,0:T(8,128)(2,1)}, bf16[96,3072]{1,0:T(8,128)(2,1)}, bf16[96,3072]{1,0:T(8,128)(2,1)}, bf16[4,96,768]{2,1,0:T(8,128)(2,1)}, /*index=5*/f32[16,768]{1,0:T(8,128)}) custom-call(bf16[4,2,96,3072]{3,2,1,0:T(8,128)(2,1)} %get-tuple-element.43.g_up, bf16[4,2,4,96,768]{4,3,2,1,0:T(8,128)(2,1)} %get-tuple-element.44.g_down, ...), custom_call_target="tpu_custom_call" | custom-call | tf_op jit(solution)/shard_map/back/pallas_call | solution.py:1141
  208.6 4.5 %finish.1 = (bf16[512,768]{1,0:T(8,128)(2,1)}, bf16[512,768]{1,0:T(8,128)(2,1)}, f32[96]{0:T(128)}, f32[96]{0:T(128)}, f32[96]{0:T(128)}, /*index=5*/f32[96]{0:T...) custom-call(bf16[96,3072]{1,0:T(8,128)(2,1)} %get-tuple-element.52.f, ...), custom_call_target="tpu_custom_call" | custom-call | tf_op jit(solution)/shard_map/finish/pallas_call | solution.py:1201

commit v6 on v5

--- a/solution.py
+++ b/solution.py
@@ -47,6 +47,7 @@
 
 
 CHUNKS = tuple((g, i) for g in range(3) for i in range(3))
+LAST = len(CHUNKS) - 1
 ALL = slice(None)
 
 
@@ -88,11 +89,14 @@
     return lead + ((2, r, 256) if x_all else (r, 256 // lay.sub))
 
 
-def barrier_with(peers):
+def greet(peers):
     sem = pltpu.get_barrier_semaphore()
     for peer in peers:
         pl.semaphore_signal(sem, inc=1, device_id=peer, device_id_type=MESH)
-    pl.semaphore_wait(sem, len(peers))
+
+
+def wait_greetings(peers):
+    pl.semaphore_wait(pltpu.get_barrier_semaphore(), len(peers))
 
 
 def line_peers(lay):
@@ -206,7 +210,7 @@
 
 class Reduce:
     def __init__(self, lay, ps, fs, bufs, sems, wanted):
-        (ca, ra1, rb1, ra2, rb2, ra3) = bufs
+        (ca, ra1, rb1, ra2, rb2, ra3, rz, rx) = bufs
         (c_s, c_r, x_s, x_r, y_s, y_r, z_s, z_r, fx_s, fx_r, fc_s, fc_r) = sems
         x, c, z, y = lay.coords()
         xs, cs, zs, ys = line_peers(lay)
@@ -242,6 +246,17 @@
                 slot = rb1[g].at[0]
                 self.copies[t, 1] = along([part(ALL, ALL, k) for k in other_y], slot, ys, y_s, y_r)
                 self.adds[t, 2] = into(part(ALL, ALL, y), slot, lay.ny - 1)
+            if t == LAST:
+                self.copies[t, 2] = along([part(ALL, k, y) for k in other_z], rz, zs, z_s, z_r)
+                own = part(ALL, z, y)
+                self.adds[t, 3] = into(own, rz, lay.nz - 1)
+                self.copies[t, 3] = [
+                    remote(own, rx.at[x], x_s.at[t, k], x_r.at[t, k], peer) for k, peer in enumerate(xs)
+                ]
+                both = shard_view(lay, fs[g], g, i, c, ALL)
+                self.adds[t, 4] = functools.partial(all_sum, both, own, rx, x)
+                self.copies[t, 4] = [remote(both, both, fc_s.at[t], fc_r.at[t], cs[0])]
+                continue
             if 2 in stages and i < 2:
                 slot = ra2[g].at[i]
                 self.copies[t, 2] = along([part(x, ALL, k) for k in other_y], slot, ys, y_s, y_r)
@@ -264,13 +279,13 @@
                 self.copies[t, 5] = [remote(both, both, fc_s.at[t], fc_r.at[t], cs[0])]
 
     def settle(self, t, k):
-        if k > 0:
+        if (t, k - 1) in self.copies:
             arrive(self.copies[t, k - 1])
             if (t, k) in self.adds:
                 self.adds[t, k]()
 
     def begin(self, t, k):
-        start(self.copies[t, k])
+        start(self.copies.get((t, k), ()))
 
     def step(self, t, k):
         self.settle(t, k)
@@ -280,6 +295,11 @@
     def drain(self):
         for group in self.copies.values():
             sent(group)
+
+
+def all_sum(out, own, slots, at):
+    slots[at] = own[...]
+    set_sum(out, [slots.at[k] for k in range(slots.shape[0])])
 
 
 def set_sum(out, srcs):
@@ -314,25 +334,42 @@
 
 def front_kernel(
     lay, rows,
-    u_up, u_down, qkv, dense, tok, grad, seg, v0, v1, v2, v3, v4, v5, v6,
+    u_up, u_down, qkv_in, dense_in, tok_in, grad_in, seg, v0, v1, v2, v3, v4, v5, v6,
     g_up, g_down, p_out, prev_out, own_out, attn_hbm, vectors, up_add, att_sums,
-    small, u_att, p_att, fg_prev, fg_own, attn_out, g_att, g_small, tok_halo, seg_halo, first_all, q_s, k_s, v_s, do_s, ctx_s, ctx_t,
+    qkv, tok, grad, small, u_att, p_att, fg_prev, fg_own, attn_out, g_att, g_small, tok_halo, seg_halo, first_all, q_s, k_s, v_s, do_s, ctx_s, ctx_t,
     dq_s, dk_s, dv_s, cos_s, low_s, high_s, bias, dk_acc, dv_acc, qkv_add, s_s, w_s, d_s,
     local_sem, z_s, z_r, y_s, y_r, x_s, x_r, c_s, c_r, sm_s, sm_r, h_s, h_r, out_sem,
-    ca, ra1, rb1, rc_s, rc_r, rx_s, rx_r, ry_s, ry_r,
+    ca, ra1, rb1, rc_s, rc_r, rx_s, rx_r, ry_s, ry_r, load_sem,
 ):
     span = 3 * rows
-    r = qkv.shape[0]
+    r = qkv_in.shape[0]
     n_chunks = len(CHUNKS)
     x, c, z, y = lay.coords()
     xs, cs, zs, ys = line_peers(lay)
     total = lay.dp * lay.fsdp
+    b = lax.axis_index("dp") * lay.fsdp + lax.axis_index("fsdp")
+
+    def stream(k):
+        t = wrap(b + k, total)
+        return {"dp": t // lay.fsdp, "fsdp": lax.rem(t, lay.fsdp)}
+
+    around = [stream(2), stream(-2), stream(1), stream(-1)]
+    peers = xs + cs + zs + ys + around
+    greet(peers)
+    loads = [
+        pltpu.make_async_copy(src, dst, load_sem.at[n])
+        for n, (src, dst) in enumerate(
+            ((qkv_in, qkv), (dense_in, u_att.at[:, pl.ds(3 * D, D)]), (tok_in, tok), (grad_in, grad))
+        )
+    ]
+    start(loads)
     plan = small_plan(r)
     for (row, size, _), ref in zip(plan, (v0, v1, v2, v3, v4, v5, v6)):
         value = ref[...].astype(F32).reshape(1, size)
         for k in range(-(-size // LANES)):
             width = min(LANES, size - k * LANES)
             small[row + k : row + k + 1, :width] = value[:, k * LANES : k * LANES + width]
+    loads[0].wait()
     left = lax.broadcasted_iota(jnp.int32, (r, LANES), 1) < HD
     for p in range(PAIRS):
         parts = [qkv[:, (3 * p + k) * LANES : (3 * p + k + 1) * LANES].astype(F32) for k in range(3)]
@@ -343,14 +380,8 @@
         )
         for k, part in enumerate(kinds):
             u_att[:, k * D + p * LANES : k * D + (p + 1) * LANES] = part.astype(BF)
-    u_att[:, 3 * D :] = dense[...]
-    b = lax.axis_index("dp") * lay.fsdp + lax.axis_index("fsdp")
-
-    def stream(k):
-        t = wrap(b + k, total)
-        return {"dp": t // lay.fsdp, "fsdp": lax.rem(t, lay.fsdp)}
-
-    around = [stream(2), stream(-2), stream(1), stream(-1)]
+    for copy in loads[1:]:
+        copy.wait()
     gs = (g_att, g_up, g_down)
     us = (u_att, u_up, u_down)
     locals_ = []
@@ -362,7 +393,7 @@
         )
     locals_.append(pltpu.make_async_copy(small, g_small.at[z, y], local_sem.at[n_chunks]))
     start(locals_)
-    barrier_with(xs + cs + zs + ys + around)
+    wait_greetings(peers)
     even = lax.rem(b, 2) == 0
     half = rows // 2
     halo, own, passed = [], [], []
@@ -673,7 +704,7 @@
     lax.fori_loop(0, PAIRS, pair, 0)
 
     sums = Reduce(
-        lay, (p_att,), None, ((ca,), (ra1,), (rb1,), None, None, None),
+        lay, (p_att,), None, ((ca,), (ra1,), (rb1,), None, None, None, None, None),
         (rc_s, rc_r, rx_s, rx_r, ry_s, ry_r) + (None,) * 6, {0: (0, 1), 1: (0,), 2: (0, 1)},
     )
     outs = []
@@ -786,10 +817,10 @@
         functools.partial(front_kernel, lay, rows),
         name="front",
         out_shape=outs,
-        in_specs=hbm(2) + [vmem] * (5 + len(vectors)),
+        in_specs=hbm(6) + [vmem] * (1 + len(vectors)),
         out_specs=tuple(hbm(6)) + (vmem,) * 3,
         scratch_shapes=[
-            v((SMALL_ROWS, LANES), F32), v((r, 4 * D)), v(grad_shape(lay, 0, r)), v((2 * rows, D)), v((rows, D), F32), v((rows, D), F32),
+            v((r, 3 * D)), v((rows, D)), v((rows, D)), v((SMALL_ROWS, LANES), F32), v((r, 4 * D)), v(grad_shape(lay, 0, r)), v((2 * rows, D)), v((rows, D), F32), v((rows, D), F32),
             v(grad_shape(lay, 0, r)), v((lay.nz, lay.ny, SMALL_ROWS, LANES), F32), v((2, rows, D)),
             v((2, 1, rows), jnp.int32), v((span, D)), v((rows, D)), v((span, D)),
             v((span, D)), v((rows, D)), v((rows, D)), v((D, rows)), v((rows, D)), v((span, D)),
@@ -801,7 +832,7 @@
             v((3,) + part_shape(lay, 0, True, True, True, r)),
             v((1, lx) + part_shape(lay, 0, False, True, True, r)),
             v((1, ly) + part_shape(lay, 0, True, True, False, r)),
-            dma(3), dma(3), dma(3, lx), dma(3, lx), dma(3, ly), dma(3, ly),
+            dma(3), dma(3), dma(3, lx), dma(3, lx), dma(3, ly), dma(3, ly), dma(4),
         ],
         compiler_params=pltpu.CompilerParams(
             collective_id=0, has_side_effects=True, vmem_limit_bytes=VMEM_LIMIT
@@ -823,10 +854,10 @@
 
 def back_kernel(
     lay, rows, docs,
-    g_up, g_down, p_in, prev_in, own_in, attn_in, vectors, up_add, att_sums, tok, grad, seg,
+    g_up, g_down, p_in, prev_in, own_in, attn_in, tok_in, grad_in, vectors, up_add, att_sums, seg,
     out_hbm, input_hbm, att_hbm, up_hbm, down_hbm, vec_out,
-    output, input_grad, f_att, f_up, f_down, p_att, fg_prev, fg_own, attn_out, p_up, p_down, w_up, w_down, second_in, second_t, act_s, pg_s, sg_acc, hop, home,
-    ca, ra1, rb1, ra2, rb2, ra3, v_c, v_x, v_y, v_z, *sems,
+    tok, grad, output, input_grad, f_att, f_up, f_down, p_att, fg_prev, fg_own, attn_out, p_up, p_down, w_up, w_down, second_in, second_t, act_s, pg_s, sg_acc, hop, home,
+    ca, ra1, rb1, ra2, rb2, ra3, rz, rx, v_c, v_x, v_y, v_z, *sems,
 ):
     (c_s, c_r, x_s, x_r, y_s, y_r, z_s, z_r, fx_s, fx_r, fc_s, fc_r, v_s, v_r, w_sem, h_s, h_r, in_sem, out_sem) = sems
     r = p_in.shape[2]
@@ -854,6 +885,8 @@
                 ),
             )
         )
+    peers = xs + cs + zs + ys + around
+    greet(peers)
     taken = [
         pltpu.make_async_copy(
             p_in.at[:, :, :, pl.ds(1024 * i, 1024)], p_att.at[:, :, :, pl.ds(1024 * i, 1024)],
@@ -864,16 +897,19 @@
     taken.append(pltpu.make_async_copy(prev_in, fg_prev, in_sem.at[3]))
     taken.append(pltpu.make_async_copy(attn_in, attn_out, in_sem.at[4]))
     taken.append(pltpu.make_async_copy(own_in, fg_own, in_sem.at[5]))
+    taken.append(pltpu.make_async_copy(tok_in, tok, in_sem.at[6]))
+    taken.append(pltpu.make_async_copy(grad_in, grad, in_sem.at[7]))
     start(taken[:4])
+    start(taken[6:])
     start(loads[0])
-    start(taken[4:])
+    start(taken[4:6])
     start(loads[1])
-    barrier_with(xs + cs + zs + ys + around)
+    wait_greetings(peers)
     wanted = {t: (0, 1, 2, 3) for t in range(3, len(CHUNKS))}
     wanted.update({0: (2, 3), 1: (1, 2, 3), 2: (2, 3)})
     net = Reduce(
         lay, (p_att, p_up, p_down), (f_att, f_up, f_down),
-        ((None,) + tuple(ca), ra1, (None,) + tuple(rb1), ra2, rb2, ra3), sems[:12], wanted,
+        ((None,) + tuple(ca), ra1, (None,) + tuple(rb1), ra2, rb2, ra3, rz, rx), sems[:12], wanted,
     )
     for t, k in ((1, 1), (2, 2), (0, 2)):
         taken[t].wait()
@@ -913,6 +949,8 @@
     hop_halo(1)
 
     gain_first, gain_second = vectors[0:1, :], vectors[2:3, :]
+    taken[6].wait()
+    taken[7].wait()
     normed, factor = norm_parts(tok[...].astype(F32))
     value = (normed * gain_second + vectors[3:4, :]).astype(BF)
     second_in[...] = value
@@ -935,7 +973,7 @@
         [(step, 3, 1), (step, 2, 3), (hop_halo, 3)],
         [(step, 4, 0), (forward_halo, 1)],
         [(step, 4, 1), (step, 0, 4)],
-        [(step, 5, 0), (step, 6, 0), (step, 7, 0), (step, 8, 0), (step, 2, 4)],
+        [(step, 8, 0), (step, 6, 0), (step, 5, 0), (step, 7, 0), (step, 2, 4)],
     ]
     root = math.sqrt(0.5)
     level = 1.0 / math.sqrt(2.0 * math.pi)
@@ -989,7 +1027,7 @@
 
     squares = lax.fori_loop(0, FF_CHUNKS, chunk, jnp.zeros((rows, 1), F32))
     run = lambda *pairs: [step(t, k) for t, k in pairs]
-    run((5, 1), (6, 1), (3, 2), (1, 3))
+    run((8, 1), (6, 1), (3, 2), (1, 3))
     output[...] = output_base[...].astype(BF)
     left = []
 
@@ -1015,7 +1053,7 @@
     member = jnp.where((docs_of == doc) & (doc < docs), 1.0, 0.0)
     put(12, jnp.sum(token_norm * member, 0, keepdims=True))
     put(13, jnp.sum(member, 0, keepdims=True))
-    run((4, 2), (5, 2), (7, 1), (8, 1), (1, 4))
+    run((4, 2), (5, 1), (7, 1), (8, 2), (1, 4))
     keep = jnp.where(even, 1.0, 0.0).astype(F32)
 
     def norms(k):
@@ -1040,11 +1078,12 @@
     sums = add_up(sums, norms(1))
     run((6, 2))
     sums = add_up(sums, norms(2))
+    run((4, 3))
     sums = add_up(sums, norms(3))
     leave(1, input_grad, input_hbm)
     for k in range(4):
         put(k, sums[k])
-    run((4, 3))
+    run((8, 3))
 
     at = [0, 1, lay.nx, lay.nx + lay.ny - 1]
 
@@ -1066,22 +1105,22 @@
         return value
 
     start(vec_c)
-    run((5, 3), (8, 2))
+    run((7, 2))
     arrive(vec_c)
     v_x[x] = add_all(v_c, 2)
     start(vec_x)
-    run((7, 2), (3, 4), (6, 3), (8, 3), (7, 3))
+    run((5, 2), (6, 3), (3, 4), (5, 3), (7, 3))
     arrive(vec_x)
     v_y[y] = add_all(v_x, lay.nx)
     start(vec_y)
-    run((4, 4), (5, 4))
+    run((4, 4), (8, 4))
     arrive(vec_y)
     v_z[z] = add_all(v_y, lay.ny)
     start(vec_z)
-    run((6, 4), (0, 5), (1, 5), (2, 5), (3, 5), (4, 5), (5, 5), (8, 4))
+    run((0, 5), (1, 5), (2, 5), (3, 5), (4, 5), (6, 4), (5, 4), (6, 5), (5, 5))
     run((0, 6), (1, 6), (2, 6))
     leave(2, f_att, att_hbm)
-    run((6, 5), (3, 6), (4, 6), (5, 6), (7, 4))
+    run((7, 4), (3, 6), (4, 6), (5, 6))
     leave(3, f_up, up_hbm)
     arrive(vec_z)
     vec_out[...] = add_all(v_z, lay.nz)
@@ -1118,7 +1157,7 @@
         ]
 
     scratch = [
-        v((rows, D)), v((rows, D)), v((r, 4 * D)), v((r, 4 * D)), v((4, r, D)),
+        v((rows, D)), v((rows, D)), v((rows, D)), v((rows, D)), v((r, 4 * D)), v((r, 4 * D)), v((4, r, D)),
         v(grad_shape(lay, 0, r)), v((2 * rows, D)), v((rows, D), F32), v((rows, D), F32),
         v(grad_shape(lay, 1, r)), v(grad_shape(lay, 2, r)),
         v((2, lay.nz, lay.ny, r, D)), v((2, lay.nz // FF_CHUNKS, lay.ny, 4, r, D)),
@@ -1130,25 +1169,27 @@
         bufs(2, (ly,), False, True, False),
         bufs(1, (lx,), False, True, False),
         bufs(3, (lz,), False, False, False),
+        v((lz,) + part_shape(lay, 2, True, False, False, r)),
+        v((lay.nx,) + part_shape(lay, 2, True, False, False, r)),
     ]
     vecs = [v((k, 16, D), F32) for k in (2, lay.nx, lay.ny, lay.nz)]
     nv = 1 + lay.nx + lay.ny + lay.nz
     sems = [
         dma(n), dma(n), dma(n, lx), dma(n, lx), dma(n, ly), dma(n, ly), dma(n, lz), dma(n, lz),
-        dma(n, lx), dma(n, lx), dma(n), dma(n), dma(nv), dma(nv), dma(2, FF_CHUNKS), dma(8), dma(8), dma(6), dma(5),
+        dma(n, lx), dma(n, lx), dma(n), dma(n), dma(nv), dma(nv), dma(2, FF_CHUNKS), dma(8), dma(8), dma(8), dma(5),
     ]
     vmem = pl.BlockSpec(memory_space=pltpu.VMEM)
     return pl.pallas_call(
         functools.partial(back_kernel, lay, rows, docs),
         name="back",
         out_shape=outs,
-        in_specs=hbm(6) + [vmem] * 6,
+        in_specs=hbm(8) + [vmem] * 4,
         out_specs=tuple(hbm(5)) + (vmem,),
         scratch_shapes=scratch + vecs + sems,
         compiler_params=pltpu.CompilerParams(
             collective_id=1, has_side_effects=True, vmem_limit_bytes=VMEM_LIMIT
         ),
-    )(g_up, g_down, p_att, fg_prev, fg_own, attn_out, vectors, up_add, att_sums, tok, grad, seg)
+    )(g_up, g_down, p_att, fg_prev, fg_own, attn_out, tok, grad, vectors, up_add, att_sums, seg)
 
 
 def finish_kernel(

time: 213 us -> 211 us (level)
  no operation moved by 1% of the time
where the time goes in v6:
time: 211 us
  Pallas kernels  210 us (100%)
    pallas_call x1, Pallas kernels, front(): pl.pallas_call(functools.partial(front_kernel, lay, rows), name='front',...  118 us
    pallas_call x1, Pallas kernels, back(): pl.pallas_call(functools.partial(back_kernel, lay, rows, docs), name='bac...  87.6 us
    pallas_call x1, Pallas kernels, finish(): pl.pallas_call(functools.partial(finish_kernel, lay, docs, r), name='fini...  4.46 us

profile of v6, /device:TPU:1, one launch (start us, length us, event | category | flops | bytes accessed | tf_op | source)
XLA Modules:
  0.0 211.2 jit_solution(13382586312367382289)
XLA Ops:
  0.6 118.4 %front.1 = (bf16[4,2,96,3072]{3,2,1,0:T(8,128)(2,1)}, bf16[4,2,4,96,768]{4,3,2,1,0:T(8,128)(2,1)}, bf16[4,2,96,3072]{3,2,1,0:T(8,128)(2,1)}, bf16[1024,768]{1,0:...) custom-call(bf16[96,3072]{1,0:T(8,128)(2,1)} %u_up.1, ...), custom_call_target="tpu_custom_call" | custom-call | tf_op jit(solution)/shard_map/front/pallas_call | solution.py:816
  119.0 87.6 %back.1 = (bf16[512,768]{1,0:T(8,128)(2,1)}, bf16[512,768]{1,0:T(8,128)(2,1)}, bf16[96,3072]{1,0:T(8,128)(2,1)}, bf16[96,3072]{1,0:T(8,128)(2,1)}, bf16[4,96,768]{2,1,0:T(8,128)(2,1)}, /*index=5*/f32[16,768]{1,0:T(8,128)}) custom-call(bf16[4,2,96,3072]{3,2,1,0:T(8,128)(2,1)} %get-tuple-element.43.g_up, bf16[4,2,4,96,768]{4,3,2,1,0:T(8,128)(2,1)} %get-tuple-element.44.g_down, ...), custom_call_target="tpu_custom_call" | custom-call | tf_op jit(solution)/shard_map/back/pallas_call | solution.py:1182
  206.6 4.5 %finish.1 = (bf16[512,768]{1,0:T(8,128)(2,1)}, bf16[512,768]{1,0:T(8,128)(2,1)}, f32[96]{0:T(128)}, f32[96]{0:T(128)}, f32[96]{0:T(128)}, /*index=5*/f32[96]{0:T...) custom-call(bf16[96,3072]{1,0:T(8,128)(2,1)} %get-tuple-element.52.f, ...), custom_call_target="tpu_custom_call" | custom-call | tf_op jit(solution)/shard_map/finish/pallas_call | solution.py:1242

commit v7 on v6

--- a/solution.py
+++ b/solution.py
@@ -1105,11 +1105,11 @@
         return value
 
     start(vec_c)
-    run((7, 2))
+    run((5, 2))
     arrive(vec_c)
     v_x[x] = add_all(v_c, 2)
     start(vec_x)
-    run((5, 2), (6, 3), (3, 4), (5, 3), (7, 3))
+    run((7, 2), (6, 3), (5, 3), (3, 4), (7, 3))
     arrive(vec_x)
     v_y[y] = add_all(v_x, lay.nx)
     start(vec_y)

time: 211 us -> 210 us (level)
  no operation moved by 1% of the time
where the time goes in v7:
time: 210 us
  Pallas kernels  209 us (100%)
    pallas_call x1, Pallas kernels, front(): pl.pallas_call(functools.partial(front_kernel, lay, rows), name='front',...  118 us
    pallas_call x1, Pallas kernels, back(): pl.pallas_call(functools.partial(back_kernel, lay, rows, docs), name='bac...  86.5 us
    pallas_call x1, Pallas kernels, finish(): pl.pallas_call(functools.partial(finish_kernel, lay, docs, r), name='fini...  4.46 us

profile of v7, /device:TPU:1, one launch (start us, length us, event | category | flops | bytes accessed | tf_op | source)
XLA Modules:
  0.0 210.2 jit_solution(12447030777147196946)
XLA Ops:
  0.6 118.4 %front.1 = (bf16[4,2,96,3072]{3,2,1,0:T(8,128)(2,1)}, bf16[4,2,4,96,768]{4,3,2,1,0:T(8,128)(2,1)}, bf16[4,2,96,3072]{3,2,1,0:T(8,128)(2,1)}, bf16[1024,768]{1,0:...) custom-call(bf16[96,3072]{1,0:T(8,128)(2,1)} %u_up.1, ...), custom_call_target="tpu_custom_call" | custom-call | tf_op jit(solution)/shard_map/front/pallas_call | solution.py:816
  119.0 86.5 %back.1 = (bf16[512,768]{1,0:T(8,128)(2,1)}, bf16[512,768]{1,0:T(8,128)(2,1)}, bf16[96,3072]{1,0:T(8,128)(2,1)}, bf16[96,3072]{1,0:T(8,128)(2,1)}, bf16[4,96,768]{2,1,0:T(8,128)(2,1)}, /*index=5*/f32[16,768]{1,0:T(8,128)}) custom-call(bf16[4,2,96,3072]{3,2,1,0:T(8,128)(2,1)} %get-tuple-element.43.g_up, bf16[4,2,4,96,768]{4,3,2,1,0:T(8,128)(2,1)} %get-tuple-element.44.g_down, ...), custom_call_target="tpu_custom_call" | custom-call | tf_op jit(solution)/shard_map/back/pallas_call | solution.py:1182
  205.5 4.5 %finish.1 = (bf16[512,768]{1,0:T(8,128)(2,1)}, bf16[512,768]{1,0:T(8,128)(2,1)}, f32[96]{0:T(128)}, f32[96]{0:T(128)}, f32[96]{0:T(128)}, /*index=5*/f32[96]{0:T...) custom-call(bf16[96,3072]{1,0:T(8,128)(2,1)} %get-tuple-element.52.f, ...), custom_call_target="tpu_custom_call" | custom-call | tf_op jit(solution)/shard_map/finish/pallas_call | solution.py:1242

commit v8 on v7

--- a/solution.py
+++ b/solution.py
@@ -597,8 +597,8 @@
         [(go, 5, 3), (go, 6, 1), (go, 3, 3), (go, 7, 1)],
         [(go, 8, 2), (go, 6, 2)],
         [(go, 4, 3), (go, 7, 2)],
-        [(go, 8, 3), (go, 6, 3)],
-        [(go, 7, 3)],
+        [(go, 8, 3)],
+        [(go, 6, 3)],
     ]
     tile = 256
 
@@ -738,6 +738,7 @@
         weight_grad(kind, j)
     sums.step(0, 1)
     sums.step(2, 0)
+    net.pass_on(7, 3)
     for kind, j in ((1, 1), (1, 2)):
         weight_grad(kind, j)
     sums.step(2, 1)

time: 210 us -> 210 us (level)
  no operation moved by 1% of the time
where the time goes in v8:
time: 210 us
  Pallas kernels  209 us (100%)
    pallas_call x1, Pallas kernels, front(): pl.pallas_call(functools.partial(front_kernel, lay, rows), name='front',...  118 us
    pallas_call x1, Pallas kernels, back(): pl.pallas_call(functools.partial(back_kernel, lay, rows, docs), name='bac...  86.3 us
    pallas_call x1, Pallas kernels, finish(): pl.pallas_call(functools.partial(finish_kernel, lay, docs, r), name='fini...  4.46 us

profile of v8, /device:TPU:1, one launch (start us, length us, event | category | flops | bytes accessed | tf_op | source)
XLA Modules:
  0.0 209.7 jit_solution(7215823561185350553)
XLA Ops:
  0.6 118.1 %front.1 = (bf16[4,2,96,3072]{3,2,1,0:T(8,128)(2,1)}, bf16[4,2,4,96,768]{4,3,2,1,0:T(8,128)(2,1)}, bf16[4,2,96,3072]{3,2,1,0:T(8,128)(2,1)}, bf16[1024,768]{1,0:...) custom-call(bf16[96,3072]{1,0:T(8,128)(2,1)} %u_up.1, ...), custom_call_target="tpu_custom_call" | custom-call | tf_op jit(solution)/shard_map/front/pallas_call | solution.py:817
  118.7 86.3 %back.1 = (bf16[512,768]{1,0:T(8,128)(2,1)}, bf16[512,768]{1,0:T(8,128)(2,1)}, bf16[96,3072]{1,0:T(8,128)(2,1)}, bf16[96,3072]{1,0:T(8,128)(2,1)}, bf16[4,96,768]{2,1,0:T(8,128)(2,1)}, /*index=5*/f32[16,768]{1,0:T(8,128)}) custom-call(bf16[4,2,96,3072]{3,2,1,0:T(8,128)(2,1)} %get-tuple-element.43.g_up, bf16[4,2,4,96,768]{4,3,2,1,0:T(8,128)(2,1)} %get-tuple-element.44.g_down, ...), custom_call_target="tpu_custom_call" | custom-call | tf_op jit(solution)/shard_map/back/pallas_call | solution.py:1183
  205.1 4.5 %finish.1 = (bf16[512,768]{1,0:T(8,128)(2,1)}, bf16[512,768]{1,0:T(8,128)(2,1)}, f32[96]{0:T(128)}, f32[96]{0:T(128)}, f32[96]{0:T(128)}, /*index=5*/f32[96]{0:T...) custom-call(bf16[96,3072]{1,0:T(8,128)(2,1)} %get-tuple-element.52.f, ...), custom_call_target="tpu_custom_call" | custom-call | tf_op jit(solution)/shard_map/finish/pallas_call | solution.py:1243
